TPU v7x, 256 devices: a whole 4x4x8 slice. The times are simulated.
256 devices in a mesh: panel: 2 (over y_hi), colat: 4 (over y_lo, core), lon: 32 (over x, z).
Axes of the slice: x: 4, y: 4 (y_hi: 2, y_lo: 2; y = y_hi * 2 + y_lo), z: 8, core: 2. Of those that a mesh axis runs over, the one named last changes fastest.
Arguments:
- heat_anomaly: float32 [2, 8, 128, 4096], P('panel', None, 'colat', 'lon'), may hold values from -6 to 6
- prior_flow: float32 [2, 3, 8, 128, 4096], P('panel', None, None, 'colat', 'lon'), may hold values from -6 to 6
- stiffness_profile: float32 [8], replicated, may hold values from 1 to 30
- source_site_lookup: int32 [2, 4, 20480], P('panel', 'colat', 'lon'), may hold values from 0 to 4095
- frame_turning_phase: float32 [2, 4, 10240], P('panel', 'colat', 'lon'), may hold values from -3.140625 to 3.140625
Outputs:
- heat_after_step: float32 [2, 8, 128, 4096], P('panel', None, 'colat', 'lon')
- new_velocity: float32 [2, 3, 8, 128, 4096], P('panel', None, None, 'colat', 'lon')
Inputs may be any that keep to these rules, and one draw needn't show every extreme that they name: `source_site_lookup`: a flat cell of the donor tile, row times 128 plus column.
All inputs are finite; a program needn't handle non-finite values.
Results may differ from a plain program's by a relative error of at most 0.00002.
Values sent between devices are 32-bit elements; how exact they have to be, the bound alone decides.
A program may use at most 64 MiB of HBM per device.

v0:
```python
import jax
import jax.numpy as jnp
from jax import lax
from jax.sharding import PartitionSpec as P

ITERS = 8


TIME_STEP = 0.1
BUOYANCY_FACTOR = 10.0
DRAG_COEF = 1.0


def swapped(value, axis, stride):
    mask = 2**stride
    pairs = [(source, source ^ mask) for source in range(lax.axis_size(axis))]
    return lax.ppermute(value, axis, pairs)


def with_halo(shard, sides, width):
    for axis, dim in sides:
        size, length = (lax.axis_size(axis), shard.shape[dim])
        up = [(i, (i + 1) % size) for i in range(size - 1)]
        down = [(j, i) for i, j in up]
        last = lax.slice_in_dim(shard, length - width, length, axis=dim)
        first = lax.slice_in_dim(shard, 0, width, axis=dim)
        before = lax.ppermute(last, axis, up)
        after = lax.ppermute(first, axis, down)
        shard = jnp.concatenate([before, shard, after], axis=dim)
    return shard


def march_heat_state(framed_array, arriving_flow):
    centre_val = framed_array[..., 2:-2, 2:-2]
    grad_colat = (
        8.0 * (framed_array[..., 3:-1, 2:-2] - framed_array[..., 1:-3, 2:-2])
        - (framed_array[..., 4:, 2:-2] - framed_array[..., :-4, 2:-2])
    ) / 12.0
    grad_lon = (
        8.0 * (framed_array[..., 2:-2, 3:-1] - framed_array[..., 2:-2, 1:-3])
        - (framed_array[..., 2:-2, 4:] - framed_array[..., 2:-2, :-4])
    ) / 12.0
    level_above = jnp.concatenate([centre_val[..., 1:, :, :], centre_val[..., -1:, :, :]], axis=-3)
    level_below = jnp.concatenate([centre_val[..., :1, :, :], centre_val[..., :-1, :, :]], axis=-3)
    grad_rad = (level_above - level_below) / 2.0
    laplace = (
        framed_array[..., 3:-1, 2:-2]
        + framed_array[..., 1:-3, 2:-2]
        + framed_array[..., 2:-2, 3:-1]
        + framed_array[..., 2:-2, 1:-3]
        + level_above
        + level_below
        - 6.0 * centre_val
    )
    advect = (
        arriving_flow[..., 0, :, :, :] * grad_rad
        + arriving_flow[..., 1, :, :, :] * grad_colat
        + arriving_flow[..., 2, :, :, :] * grad_lon
    )
    return centre_val + TIME_STEP * (laplace - advect)


def coefficients(stiffness_profile):
    interface = 0.5 * (stiffness_profile[:-1] + stiffness_profile[1:])
    zero_pad = jnp.zeros_like(stiffness_profile[:1])
    upper_coef = jnp.concatenate([interface, zero_pad])
    lower_coef = jnp.concatenate([zero_pad, interface])
    diagonal = DRAG_COEF + 4.0 * stiffness_profile + upper_coef + lower_coef
    return (upper_coef, lower_coef, diagonal)


def neighbours(framed_array):
    return (
        framed_array[..., 2:, 1:-1]
        + framed_array[..., :-2, 1:-1]
        + framed_array[..., 1:-1, 2:]
        + framed_array[..., 1:-1, :-2]
    )


def sweep(field_in, near_sum, buoyancy_source, stiffness_profile, upper_coef, lower_coef, diagonal):
    col_shape = (stiffness_profile.shape[0], 1, 1)
    zero_level = jnp.zeros_like(field_in[..., :1, :, :])
    level_above = jnp.concatenate([field_in[..., 1:, :, :], zero_level], axis=-3)
    level_below = jnp.concatenate([zero_level, field_in[..., :-1, :, :]], axis=-3)
    numerator = (
        buoyancy_source
        + stiffness_profile.reshape(col_shape) * near_sum
        + upper_coef.reshape(col_shape) * level_above
        + lower_coef.reshape(col_shape) * level_below
    )
    return numerator / diagonal.reshape(col_shape)


def rotate(values, cos_term, sine_term):
    first = values[..., 1, :, :]
    second = values[..., 2, :, :]
    return jnp.stack(
        [
            values[..., 0, :, :],
            cos_term * first + sine_term * second,
            cos_term * second - sine_term * first,
        ],
        axis=-3,
    )


def inner_slots(source_site_position, patch_height, patch_breadth):
    base = 4 * patch_breadth
    return jnp.concatenate(
        [
            source_site_position[..., patch_breadth : 2 * patch_breadth],
            source_site_position[..., 2 * patch_breadth : 3 * patch_breadth],
            source_site_position[..., base + 1 : base + 2 * patch_height : 2],
            source_site_position[..., base + 2 * patch_height : base + 4 * patch_height : 2],
        ],
        axis=-1,
    )


def fill_wide(framed_array, obtained_broad_strip, flags, patch_height, patch_breadth):
    depth_count = obtained_broad_strip.shape[0]
    base = 4 * patch_breadth
    north_rim = obtained_broad_strip[:, 0 : 2 * patch_breadth].reshape(
        depth_count, 2, patch_breadth
    )
    south_rim = obtained_broad_strip[:, 2 * patch_breadth : base].reshape(
        depth_count, 2, patch_breadth
    )
    west_rim = obtained_broad_strip[:, base : base + 2 * patch_height].reshape(
        depth_count, patch_height, 2
    )
    east_rim = obtained_broad_strip[:, base + 2 * patch_height :].reshape(
        depth_count, patch_height, 2
    )
    framed_array = framed_array.at[:, 0:2, 2 : patch_breadth + 2].set(
        jnp.where(flags[0], north_rim, framed_array[:, 0:2, 2 : patch_breadth + 2])
    )
    framed_array = framed_array.at[
        :, patch_height + 2 : patch_height + 4, 2 : patch_breadth + 2
    ].set(
        jnp.where(
            flags[1],
            south_rim,
            framed_array[:, patch_height + 2 : patch_height + 4, 2 : patch_breadth + 2],
        )
    )
    framed_array = framed_array.at[:, 2 : patch_height + 2, 0:2].set(
        jnp.where(flags[2], west_rim, framed_array[:, 2 : patch_height + 2, 0:2])
    )
    framed_array = framed_array.at[
        :, 2 : patch_height + 2, patch_breadth + 2 : patch_breadth + 4
    ].set(
        jnp.where(
            flags[3],
            east_rim,
            framed_array[:, 2 : patch_height + 2, patch_breadth + 2 : patch_breadth + 4],
        )
    )
    return framed_array


def fill_thin(framed_array, got_thin, flags, patch_height, patch_breadth):
    north_rim = got_thin[..., 0:patch_breadth]
    south_rim = got_thin[..., patch_breadth : 2 * patch_breadth]
    west_rim = got_thin[..., 2 * patch_breadth : 2 * patch_breadth + patch_height]
    east_rim = got_thin[..., 2 * patch_breadth + patch_height :]
    framed_array = framed_array.at[:, :, 0, 1 : patch_breadth + 1].set(
        jnp.where(flags[0], north_rim, framed_array[:, :, 0, 1 : patch_breadth + 1])
    )
    framed_array = framed_array.at[:, :, patch_height + 1, 1 : patch_breadth + 1].set(
        jnp.where(flags[1], south_rim, framed_array[:, :, patch_height + 1, 1 : patch_breadth + 1])
    )
    framed_array = framed_array.at[:, :, 1 : patch_height + 1, 0].set(
        jnp.where(flags[2], west_rim, framed_array[:, :, 1 : patch_height + 1, 0])
    )
    framed_array = framed_array.at[:, :, 1 : patch_height + 1, patch_breadth + 1].set(
        jnp.where(flags[3], east_rim, framed_array[:, :, 1 : patch_height + 1, patch_breadth + 1])
    )
    return framed_array


def on_device(heat_anomaly, prior_flow, stiffness_profile, source_site_lookup, frame_turning_phase):
    middle_heat_value = heat_anomaly[0]
    flow_array = prior_flow[0]
    depth_count, patch_height, patch_breadth = middle_heat_value.shape
    source_site_position = source_site_lookup.reshape(-1)
    slot_angle = frame_turning_phase.reshape(-1)
    colat_pos = lax.axis_index("colat")
    lon_pos = lax.axis_index("lon")
    flags = (
        colat_pos == 0,
        colat_pos == lax.axis_size("colat") - 1,
        lon_pos == 0,
        lon_pos == lax.axis_size("lon") - 1,
    )
    dispatched_broad_strip = jnp.take(
        middle_heat_value.reshape(depth_count, -1), source_site_position, axis=1
    )
    obtained_broad_strip = swapped(dispatched_broad_strip, "panel", 0)
    broad_margin = with_halo(middle_heat_value, (("colat", 1), ("lon", 2)), 2)
    broad_margin = fill_wide(broad_margin, obtained_broad_strip, flags, patch_height, patch_breadth)
    heat_after_step = march_heat_state(broad_margin, flow_array)
    upper_coef, lower_coef, diagonal = coefficients(stiffness_profile)
    blank_array = jnp.zeros_like(heat_after_step)
    buoyancy_source = jnp.stack(
        [BUOYANCY_FACTOR * heat_after_step, blank_array, blank_array], axis=0
    )
    inner_index = inner_slots(source_site_position, patch_height, patch_breadth)
    cos_term = jnp.cos(slot_angle)[None, :]
    sine_term = jnp.sin(slot_angle)[None, :]
    for sweep_no in range(ITERS):
        sent_thin = rotate(
            jnp.take(flow_array.reshape(3, depth_count, -1), inner_index, axis=2),
            cos_term,
            sine_term,
        )
        got_thin = swapped(sent_thin, "panel", 0)
        thin = with_halo(flow_array, (("colat", 2), ("lon", 3)), 1)
        thin = fill_thin(thin, got_thin, flags, patch_height, patch_breadth)
        near_sum = neighbours(thin)
        flow_array = sweep(
            flow_array,
            near_sum,
            buoyancy_source,
            stiffness_profile,
            upper_coef,
            lower_coef,
            diagonal,
        )
    return (heat_after_step[None], flow_array[None])


def solution(mesh):
    return jax.shard_map(
        on_device,
        mesh=mesh,
        in_specs=(
            P("panel", None, "colat", "lon"),
            P("panel", None, None, "colat", "lon"),
            P(),
            P("panel", "colat", "lon"),
            P("panel", "colat", "lon"),
        ),
        out_specs=(P("panel", None, "colat", "lon"), P("panel", None, None, "colat", "lon")),
        check_vma=False,
    )
```

profile of v0, /device:TPU:6, one launch (start us, length us, event | category | flops | bytes accessed | tf_op | source)
XLA Modules:
  0.0 471.0 jit_solution(16224185562006067157)
XLA Ops:
  2.5 5.8 %copy.6093 = f32[1,3,8,32,128]{2,1,4,3,0:T(4,128)} copy(f32[1,3,8,32,128]{4,3,2,1,0:T(8,128)} %param.80) | data formatting | bytes 786432 | tf_op args[1]
  8.3 4.5 gather_fusion.1
  20.9 4.4 collective-permute-start
  35.1 3.8 collective-permute-start.2
  39.0 6.1 %collective-permute-start.3 = (f32[8,36,2]{2,0,1:T(8,128)S(1)}, f32[8,36,2]{2,0,1:T(8,128)S(1)}, u32[]{:S(2)}, u32[]{:S(2)}) collective-permute-start(f32[8,36,2]{2,0,1:T(8,128)S(1)} %get-tuple-element.564), channel_id=1, source_target_pairs={{1,0},{2,1},{3,2},{4,3},{5,4},{6,5},{7,6},{8,7},{9,8},{10,9},{11,1... | collective-permute-start | bytes 6920 | tf_op jit(solution)/shard_map/ppermute | solution.py:28
  47.3 6.2 %collective-permute-start.8 = (f32[3,8,34,1]{3,1,2,0:T(8,128)S(1)}, f32[3,8,34,1]{3,1,2,0:T(8,128)S(1)}, u32[]{:S(2)}, u32[]{:S(2)}) collective-permute-start(f32[3,8,34,1]{3,1,2,0:T(8,128)S(1)} %get-tuple-element.522), channel_id=1, source_target_pairs={{1,0},{2,1},{3,2},{4,3},{5,4},{6,5},{7,6},{8,7},{9,8},{10,9},{11,1... | collective-permute-start | bytes 9800 | tf_op jit(solution)/shard_map/ppermute | solution.py:28
  53.8 7.8 %collective-permute-done.7 = f32[3,8,34,1]{3,1,2,0:T(8,128)S(1)} collective-permute-done((f32[3,8,34,1]{3,1,2,0:T(8,128)S(1)}, f32[3,8,34,1]{3,1,2,0:T(8,128)S(1)}, u32[]{:S(2)}, u32[]{:S(2)}) %collective-permute-start.7) | collective-permute-done | bytes 3296 | tf_op jit(solution)/shard_map/ppermute | solution.py:27
  65.8 4.0 scatter.120
  82.8 3.6 scatter.130
  87.1 9.9 %scatter.131 = f32[3,8,34,130]{3,1,0,2:T(8,128)S(1)} dynamic-update-slice(f32[3,8,34,130]{3,1,0,2:T(8,128)S(1)} %scatter.130, f32[3,8,32,1]{3,1,0,2:T(8,128)S(1)} %copy.6103, s32[]{:T(128)} %constant.870.clone.1, s32[]{:T(128)} %constant.870.clone.1, s32[]{:T(128)} %constant.893.clone.1, s32[]{:T(128)} %constant.894.clone.1) | dynamic-update-slice | bytes 6148 | tf_op jit(solution)/shard_map/scatter | solution.py:177
  97.4 5.7 %copy.6230 = f32[3,8,32,128]{1,0,3,2:T(4,128)} copy(f32[3,8,32,128]{3,1,0,2:T(8,128)S(1)} %fusion.2) | data formatting | bytes 786432 | tf_op jit(solution)/shard_map/reshape | solution.py:214
  103.2 4.5 gather_fusion.2
  115.1 6.5 %collective-permute-start.13 = (f32[3,8,34,1]{3,1,2,0:T(8,128)S(1)}, f32[3,8,34,1]{3,1,2,0:T(8,128)S(1)}, u32[]{:S(2)}, u32[]{:S(2)}) collective-permute-start(f32[3,8,34,1]{3,1,2,0:T(8,128)S(1)} %get-tuple-element.520), channel_id=1, source_target_pairs={{1,0},{2,1},{3,2},{4,3},{5,4},{6,5},{7,6},{8,7},{9,8},{10,9},{11,1... | collective-permute-start | bytes 9800 | tf_op jit(solution)/shard_map/ppermute | solution.py:28
  123.7 5.2 %collective-permute-done.12 = f32[3,8,34,1]{3,1,2,0:T(8,128)S(1)} collective-permute-done((f32[3,8,34,1]{3,1,2,0:T(8,128)S(1)}, f32[3,8,34,1]{3,1,2,0:T(8,128)S(1)}, u32[]{:S(2)}, u32[]{:S(2)}) %collective-permute-start.12) | collective-permute-done | bytes 3296 | tf_op jit(solution)/shard_map/ppermute | solution.py:27
  135.3 3.6 scatter.136
  139.6 9.9 %scatter.139 = f32[3,8,34,130]{3,1,0,2:T(8,128)S(1)} dynamic-update-slice(f32[3,8,34,130]{3,1,0,2:T(8,128)S(1)} %scatter.136, f32[3,8,32,1]{3,1,0,2:T(8,128)S(1)} %copy.6120, s32[]{:T(128)} %constant.870.clone.1, s32[]{:T(128)} %constant.870.clone.1, s32[]{:T(128)} %constant.893.clone.1, s32[]{:T(128)} %constant.894.clone.1) | dynamic-update-slice | bytes 6148 | tf_op jit(solution)/shard_map/scatter | solution.py:177
  149.9 5.7 %copy.6233 = f32[3,8,32,128]{1,0,3,2:T(4,128)} copy(f32[3,8,32,128]{3,1,0,2:T(8,128)S(1)} %fusion.5) | data formatting | bytes 786432 | tf_op jit(solution)/shard_map/reshape | solution.py:214
  155.7 4.5 gather_fusion.3
  169.4 5.6 %collective-permute-start.18 = (f32[3,8,34,1]{3,1,2,0:T(8,128)S(1)}, f32[3,8,34,1]{3,1,2,0:T(8,128)S(1)}, u32[]{:S(2)}, u32[]{:S(2)}) collective-permute-start(f32[3,8,34,1]{3,1,2,0:T(8,128)S(1)} %get-tuple-element.518), channel_id=1, source_target_pairs={{1,0},{2,1},{3,2},{4,3},{5,4},{6,5},{7,6},{8,7},{9,8},{10,9},{11,1... | collective-permute-start | bytes 9800 | tf_op jit(solution)/shard_map/ppermute | solution.py:28
  177.2 5.0 %collective-permute-done.17 = f32[3,8,34,1]{3,1,2,0:T(8,128)S(1)} collective-permute-done((f32[3,8,34,1]{3,1,2,0:T(8,128)S(1)}, f32[3,8,34,1]{3,1,2,0:T(8,128)S(1)}, u32[]{:S(2)}, u32[]{:S(2)}) %collective-permute-start.17) | collective-permute-done | bytes 3296 | tf_op jit(solution)/shard_map/ppermute | solution.py:27
  193.0 9.9 %scatter.145 = f32[3,8,34,130]{3,1,0,2:T(8,128)S(1)} dynamic-update-slice(f32[3,8,34,130]{3,1,0,2:T(8,128)S(1)} %scatter.144, f32[3,8,32,1]{3,1,0,2:T(8,128)S(1)} %copy.6137, s32[]{:T(128)} %constant.870.clone.1, s32[]{:T(128)} %constant.870.clone.1, s32[]{:T(128)} %constant.893.clone.1, s32[]{:T(128)} %constant.894.clone.1) | dynamic-update-slice | bytes 6148 | tf_op jit(solution)/shard_map/scatter | solution.py:177
  203.3 5.7 %copy.6236 = f32[3,8,32,128]{1,0,3,2:T(4,128)} copy(f32[3,8,32,128]{3,1,0,2:T(8,128)S(1)} %fusion.8) | data formatting | bytes 786432 | tf_op jit(solution)/shard_map/reshape | solution.py:214
  209.1 4.5 gather_fusion.4
  222.6 5.7 %collective-permute-start.23 = (f32[3,8,34,1]{3,1,2,0:T(8,128)S(1)}, f32[3,8,34,1]{3,1,2,0:T(8,128)S(1)}, u32[]{:S(2)}, u32[]{:S(2)}) collective-permute-start(f32[3,8,34,1]{3,1,2,0:T(8,128)S(1)} %get-tuple-element.516), channel_id=1, source_target_pairs={{1,0},{2,1},{3,2},{4,3},{5,4},{6,5},{7,6},{8,7},{9,8},{10,9},{11,1... | collective-permute-start | bytes 9800 | tf_op jit(solution)/shard_map/ppermute | solution.py:28
  230.2 5.3 %collective-permute-done.22 = f32[3,8,34,1]{3,1,2,0:T(8,128)S(1)} collective-permute-done((f32[3,8,34,1]{3,1,2,0:T(8,128)S(1)}, f32[3,8,34,1]{3,1,2,0:T(8,128)S(1)}, u32[]{:S(2)}, u32[]{:S(2)}) %collective-permute-start.22) | collective-permute-done | bytes 3296 | tf_op jit(solution)/shard_map/ppermute | solution.py:27
  246.1 9.9 %scatter.151 = f32[3,8,34,130]{3,1,0,2:T(8,128)S(1)} dynamic-update-slice(f32[3,8,34,130]{3,1,0,2:T(8,128)S(1)} %scatter.150, f32[3,8,32,1]{3,1,0,2:T(8,128)S(1)} %copy.6151, s32[]{:T(128)} %constant.870.clone.1, s32[]{:T(128)} %constant.870.clone.1, s32[]{:T(128)} %constant.893.clone.1, s32[]{:T(128)} %constant.894.clone.1) | dynamic-update-slice | bytes 6148 | tf_op jit(solution)/shard_map/scatter | solution.py:177
  256.4 5.7 %copy.6238 = f32[3,8,32,128]{1,0,3,2:T(4,128)} copy(f32[3,8,32,128]{3,1,0,2:T(8,128)S(1)} %fusion.11) | data formatting | bytes 786432 | tf_op jit(solution)/shard_map/reshape | solution.py:214
  262.2 4.5 gather_fusion.5
  275.2 6.2 %collective-permute-start.28 = (f32[3,8,34,1]{3,1,2,0:T(8,128)S(1)}, f32[3,8,34,1]{3,1,2,0:T(8,128)S(1)}, u32[]{:S(2)}, u32[]{:S(2)}) collective-permute-start(f32[3,8,34,1]{3,1,2,0:T(8,128)S(1)} %get-tuple-element.514), channel_id=1, source_target_pairs={{1,0},{2,1},{3,2},{4,3},{5,4},{6,5},{7,6},{8,7},{9,8},{10,9},{11,1... | collective-permute-start | bytes 9800 | tf_op jit(solution)/shard_map/ppermute | solution.py:28
  283.4 5.2 %collective-permute-done.27 = f32[3,8,34,1]{3,1,2,0:T(8,128)S(1)} collective-permute-done((f32[3,8,34,1]{3,1,2,0:T(8,128)S(1)}, f32[3,8,34,1]{3,1,2,0:T(8,128)S(1)}, u32[]{:S(2)}, u32[]{:S(2)}) %collective-permute-start.27) | collective-permute-done | bytes 3296 | tf_op jit(solution)/shard_map/ppermute | solution.py:27
  295.1 3.6 scatter.156
  299.4 9.9 %scatter.159 = f32[3,8,34,130]{3,1,0,2:T(8,128)S(1)} dynamic-update-slice(f32[3,8,34,130]{3,1,0,2:T(8,128)S(1)} %scatter.156, f32[3,8,32,1]{3,1,0,2:T(8,128)S(1)} %copy.6168, s32[]{:T(128)} %constant.870.clone.1, s32[]{:T(128)} %constant.870.clone.1, s32[]{:T(128)} %constant.893.clone.1, s32[]{:T(128)} %constant.894.clone.1) | dynamic-update-slice | bytes 6148 | tf_op jit(solution)/shard_map/scatter | solution.py:177
  309.7 5.7 %copy.6241 = f32[3,8,32,128]{1,0,3,2:T(4,128)} copy(f32[3,8,32,128]{3,1,0,2:T(8,128)S(1)} %fusion.14) | data formatting | bytes 786432 | tf_op jit(solution)/shard_map/reshape | solution.py:214
  315.5 4.5 gather_fusion.6
  328.5 6.2 %collective-permute-start.33 = (f32[3,8,34,1]{3,1,2,0:T(8,128)S(1)}, f32[3,8,34,1]{3,1,2,0:T(8,128)S(1)}, u32[]{:S(2)}, u32[]{:S(2)}) collective-permute-start(f32[3,8,34,1]{3,1,2,0:T(8,128)S(1)} %get-tuple-element.512), channel_id=1, source_target_pairs={{1,0},{2,1},{3,2},{4,3},{5,4},{6,5},{7,6},{8,7},{9,8},{10,9},{11,1... | collective-permute-start | bytes 9800 | tf_op jit(solution)/shard_map/ppermute | solution.py:28
  336.8 5.2 %collective-permute-done.32 = f32[3,8,34,1]{3,1,2,0:T(8,128)S(1)} collective-permute-done((f32[3,8,34,1]{3,1,2,0:T(8,128)S(1)}, f32[3,8,34,1]{3,1,2,0:T(8,128)S(1)}, u32[]{:S(2)}, u32[]{:S(2)}) %collective-permute-start.32) | collective-permute-done | bytes 3296 | tf_op jit(solution)/shard_map/ppermute | solution.py:27
  348.4 3.6 scatter.164
  352.8 9.9 %scatter.165 = f32[3,8,34,130]{3,1,0,2:T(8,128)S(1)} dynamic-update-slice(f32[3,8,34,130]{3,1,0,2:T(8,128)S(1)} %scatter.164, f32[3,8,32,1]{3,1,0,2:T(8,128)S(1)} %copy.6185, s32[]{:T(128)} %constant.870.clone.1, s32[]{:T(128)} %constant.870.clone.1, s32[]{:T(128)} %constant.893.clone.1, s32[]{:T(128)} %constant.894.clone.1) | dynamic-update-slice | bytes 6148 | tf_op jit(solution)/shard_map/scatter | solution.py:177
  363.1 5.7 %copy.6244 = f32[3,8,32,128]{1,0,3,2:T(4,128)} copy(f32[3,8,32,128]{3,1,0,2:T(8,128)S(1)} %fusion.17) | data formatting | bytes 786432 | tf_op jit(solution)/shard_map/reshape | solution.py:214
  368.9 4.5 gather_fusion.7
  381.8 6.2 %collective-permute-start.38 = (f32[3,8,34,1]{3,1,2,0:T(8,128)S(1)}, f32[3,8,34,1]{3,1,2,0:T(8,128)S(1)}, u32[]{:S(2)}, u32[]{:S(2)}) collective-permute-start(f32[3,8,34,1]{3,1,2,0:T(8,128)S(1)} %get-tuple-element.510), channel_id=1, source_target_pairs={{1,0},{2,1},{3,2},{4,3},{5,4},{6,5},{7,6},{8,7},{9,8},{10,9},{11,1... | collective-permute-start | bytes 9800 | tf_op jit(solution)/shard_map/ppermute | solution.py:28
  390.1 5.2 %collective-permute-done.37 = f32[3,8,34,1]{3,1,2,0:T(8,128)S(1)} collective-permute-done((f32[3,8,34,1]{3,1,2,0:T(8,128)S(1)}, f32[3,8,34,1]{3,1,2,0:T(8,128)S(1)}, u32[]{:S(2)}, u32[]{:S(2)}) %collective-permute-start.37) | collective-permute-done | bytes 3296 | tf_op jit(solution)/shard_map/ppermute | solution.py:27
  406.1 9.9 %scatter.171 = f32[3,8,34,130]{3,1,0,2:T(8,128)S(1)} dynamic-update-slice(f32[3,8,34,130]{3,1,0,2:T(8,128)S(1)} %scatter.170, f32[3,8,32,1]{3,1,0,2:T(8,128)S(1)} %copy.6202, s32[]{:T(128)} %constant.870.clone.1, s32[]{:T(128)} %constant.870.clone.1, s32[]{:T(128)} %constant.893.clone.1, s32[]{:T(128)} %constant.894.clone.1) | dynamic-update-slice | bytes 6148 | tf_op jit(solution)/shard_map/scatter | solution.py:177
  416.4 5.7 %copy.6247 = f32[3,8,32,128]{1,0,3,2:T(4,128)} copy(f32[3,8,32,128]{3,1,0,2:T(8,128)S(1)} %fusion.20) | data formatting | bytes 786432 | tf_op jit(solution)/shard_map/reshape | solution.py:214
  422.2 4.5 gather_fusion.8
  435.2 6.2 %collective-permute-start.43 = (f32[3,8,34,1]{3,1,2,0:T(8,128)S(1)}, f32[3,8,34,1]{3,1,2,0:T(8,128)S(1)}, u32[]{:S(2)}, u32[]{:S(2)}) collective-permute-start(f32[3,8,34,1]{3,1,2,0:T(8,128)S(1)} %get-tuple-element.508), channel_id=1, source_target_pairs={{1,0},{2,1},{3,2},{4,3},{5,4},{6,5},{7,6},{8,7},{9,8},{10,9},{11,1... | collective-permute-start | bytes 9800 | tf_op jit(solution)/shard_map/ppermute | solution.py:28
  443.2 5.5 %collective-permute-done.42 = f32[3,8,34,1]{3,1,2,0:T(8,128)S(1)} collective-permute-done((f32[3,8,34,1]{3,1,2,0:T(8,128)S(1)}, f32[3,8,34,1]{3,1,2,0:T(8,128)S(1)}, u32[]{:S(2)}, u32[]{:S(2)}) %collective-permute-start.42) | collective-permute-done | bytes 3296 | tf_op jit(solution)/shard_map/ppermute | solution.py:27
  459.4 9.9 %scatter.179 = f32[3,8,34,130]{3,1,0,2:T(8,128)S(1)} dynamic-update-slice(f32[3,8,34,130]{3,1,0,2:T(8,128)S(1)} %scatter.176, f32[3,8,32,1]{3,1,0,2:T(8,128)S(1)} %copy.6219, s32[]{:T(128)} %constant.870.clone.1, s32[]{:T(128)} %constant.870.clone.1, s32[]{:T(128)} %constant.893.clone.1, s32[]{:T(128)} %constant.894.clone.1) | dynamic-update-slice | bytes 6148 | tf_op jit(solution)/shard_map/scatter | solution.py:177
  (371 shorter events, 180.8 us)
Async XLA Ops:
  0.6 30.8 %copy-start.5 = (s32[3]{0:T(128)S(1)}, s32[3]{0:T(128)}, u32[]{:S(2)}) copy-start(s32[3]{0:T(128)} %constant.873.clone.1) | copy-start | bytes 40
  0.6 26.6 %copy-start.3 = (s32[1,1,640]{2,1,0:T(1,128)S(1)}, s32[1,1,640]{2,1,0:T(1,128)}, u32[]{:S(2)}) copy-start(s32[1,1,640]{2,1,0:T(1,128)} %param.82) | copy-start | bytes 7684
  0.7 27.2 %copy-start.2 = (f32[8]{0:T(128)S(1)}, f32[8]{0:T(128)}, u32[]{:S(2)}) copy-start(f32[8]{0:T(128)} %param.81) | copy-start | bytes 100
  13.2 65.6 %collective-permute-start.9 = (f32[3,8,320]{2,1,0:T(8,128)S(1)}, f32[3,8,320]{2,1,0:T(8,128)S(1)}, u32[]{:S(2)}, u32[]{:S(2)}) collective-permute-start(f32[3,8,320]{2,1,0:T(8,128)S(1)} %pad_maximum_fusion.20), channel_id=1, source_target_pairs={{0,128},{128,0},{1,129},{129,1},{2,130},{130,2},{3,131},{131,3},{4... | collective-permute-start | bytes 92168 | tf_op jit(solution)/shard_map/ppermute | solution.py:17
  16.7 22.3 %collective-permute-start.5 = (f32[3,8,1,128]{3,1,0,2:T(8,128)S(1)}, f32[3,8,1,128]{3,1,0,2:T(8,128)S(1)}, u32[]{:S(2)}, u32[]{:S(2)}) collective-permute-start(f32[3,8,1,128]{3,1,0,2:T(8,128)S(1)} %get-tuple-element.553), channel_id=1, source_target_pairs={{0,32},{32,64},{64,96},{1,33},{33,65},{65,97},{2,34},{34,66},{66,9... | collective-permute-start | bytes 36872 | tf_op jit(solution)/shard_map/ppermute | solution.py:27
  18.1 26.9 %collective-permute-start.6 = (f32[3,8,1,128]{3,1,0,2:T(8,128)S(1)}, f32[3,8,1,128]{3,1,0,2:T(8,128)S(1)}, u32[]{:S(2)}, u32[]{:S(2)}) collective-permute-start(f32[3,8,1,128]{3,1,0,2:T(8,128)S(1)} %get-tuple-element.554), channel_id=1, source_target_pairs={{32,0},{64,32},{96,64},{33,1},{65,33},{97,65},{34,2},{66,34},{98,6... | collective-permute-start | bytes 36872 | tf_op jit(solution)/shard_map/ppermute | solution.py:28
  19.6 15.4 %collective-permute-start.1 = (f32[8,2,128]{2,0,1:T(8,128)S(1)}, f32[8,2,128]{2,0,1:T(8,128)S(1)}, u32[]{:S(2)}, u32[]{:S(2)}) collective-permute-start(f32[8,2,128]{2,0,1:T(8,128)S(1)} %slice.1862), channel_id=1, source_target_pairs={{32,0},{64,32},{96,64},{33,1},{65,33},{97,65},{34,2},{66,34},{98,6... | collective-permute-start | bytes 24584 | tf_op jit(solution)/shard_map/ppermute | solution.py:28
  20.9 12.2 %collective-permute-start = (f32[8,2,128]{2,1,0:T(2,128)S(1)}, f32[8,2,128]{2,1,0:T(2,128)S(1)}, u32[]{:S(2)}, u32[]{:S(2)}) collective-permute-start(f32[8,2,128]{2,1,0:T(2,128)S(1)} %slice.1861), channel_id=1, source_target_pairs={{0,32},{32,64},{64,96},{1,33},{33,65},{65,97},{2,34},{34,66},{66,9... | collective-permute-start | bytes 24584 | tf_op jit(solution)/shard_map/ppermute | solution.py:27
  33.1 30.7 %collective-permute-start.4 = (f32[8,640]{0,1:T(8,128)S(1)}, f32[8,640]{0,1:T(8,128)S(1)}, u32[]{:S(2)}, u32[]{:S(2)}) collective-permute-start(f32[8,640]{0,1:T(8,128)S(1)} %select_bitcast_fusion), channel_id=1, source_target_pairs={{0,128},{128,0},{1,129},{129,1},{2,130},{130,2},{3,131},{131,3},{4... | collective-permute-start | bytes 61448 | tf_op jit(solution)/shard_map/ppermute | solution.py:17
  35.1 12.1 %collective-permute-start.2 = (f32[8,36,2]{2,0,1:T(8,128)S(1)}, f32[8,36,2]{2,0,1:T(8,128)S(1)}, u32[]{:S(2)}, u32[]{:S(2)}) collective-permute-start(f32[8,36,2]{2,0,1:T(8,128)S(1)} %get-tuple-element.563), channel_id=1, source_target_pairs={{0,1},{1,2},{2,3},{3,4},{4,5},{5,6},{6,7},{7,8},{8,9},{9,10},{10,1... | collective-permute-start | bytes 6920 | tf_op jit(solution)/shard_map/ppermute | solution.py:27
  39.0 14.6 %collective-permute-start.3 = (f32[8,36,2]{2,0,1:T(8,128)S(1)}, f32[8,36,2]{2,0,1:T(8,128)S(1)}, u32[]{:S(2)}, u32[]{:S(2)}) collective-permute-start(f32[8,36,2]{2,0,1:T(8,128)S(1)} %get-tuple-element.564), channel_id=1, source_target_pairs={{1,0},{2,1},{3,2},{4,3},{5,4},{6,5},{7,6},{8,7},{9,8},{10,9},{11,1... | collective-permute-start | bytes 6920 | tf_op jit(solution)/shard_map/ppermute | solution.py:28
  45.3 16.3 %collective-permute-start.7 = (f32[3,8,34,1]{3,1,2,0:T(8,128)S(1)}, f32[3,8,34,1]{3,1,2,0:T(8,128)S(1)}, u32[]{:S(2)}, u32[]{:S(2)}) collective-permute-start(f32[3,8,34,1]{3,1,2,0:T(8,128)S(1)} %get-tuple-element.521), channel_id=1, source_target_pairs={{0,1},{1,2},{2,3},{3,4},{4,5},{5,6},{6,7},{7,8},{8,9},{9,10},{10,1... | collective-permute-start | bytes 9800 | tf_op jit(solution)/shard_map/ppermute | solution.py:27
  47.3 16.0 %collective-permute-start.8 = (f32[3,8,34,1]{3,1,2,0:T(8,128)S(1)}, f32[3,8,34,1]{3,1,2,0:T(8,128)S(1)}, u32[]{:S(2)}, u32[]{:S(2)}) collective-permute-start(f32[3,8,34,1]{3,1,2,0:T(8,128)S(1)} %get-tuple-element.522), channel_id=1, source_target_pairs={{1,0},{2,1},{3,2},{4,3},{5,4},{6,5},{7,6},{8,7},{9,8},{10,9},{11,1... | collective-permute-start | bytes 9800 | tf_op jit(solution)/shard_map/ppermute | solution.py:28
  107.9 3.3 collective-permute-start.10
  109.9 3.1 collective-permute-start.11
  113.2 15.7 %collective-permute-start.12 = (f32[3,8,34,1]{3,1,2,0:T(8,128)S(1)}, f32[3,8,34,1]{3,1,2,0:T(8,128)S(1)}, u32[]{:S(2)}, u32[]{:S(2)}) collective-permute-start(f32[3,8,34,1]{3,1,2,0:T(8,128)S(1)} %get-tuple-element.519), channel_id=1, source_target_pairs={{0,1},{1,2},{2,3},{3,4},{4,5},{5,6},{6,7},{7,8},{8,9},{9,10},{10,1... | collective-permute-start | bytes 9800 | tf_op jit(solution)/shard_map/ppermute | solution.py:27
  115.1 15.5 %collective-permute-start.13 = (f32[3,8,34,1]{3,1,2,0:T(8,128)S(1)}, f32[3,8,34,1]{3,1,2,0:T(8,128)S(1)}, u32[]{:S(2)}, u32[]{:S(2)}) collective-permute-start(f32[3,8,34,1]{3,1,2,0:T(8,128)S(1)} %get-tuple-element.520), channel_id=1, source_target_pairs={{1,0},{2,1},{3,2},{4,3},{5,4},{6,5},{7,6},{8,7},{9,8},{10,9},{11,1... | collective-permute-start | bytes 9800 | tf_op jit(solution)/shard_map/ppermute | solution.py:28
  121.6 9.5 %collective-permute-start.14 = (f32[3,8,320]{2,1,0:T(8,128)S(1)}, f32[3,8,320]{2,1,0:T(8,128)S(1)}, u32[]{:S(2)}, u32[]{:S(2)}) collective-permute-start(f32[3,8,320]{2,1,0:T(8,128)S(1)} %pad_maximum_fusion.21), channel_id=1, source_target_pairs={{0,128},{128,0},{1,129},{129,1},{2,130},{130,2},{3,131},{131,3},{4... | collective-permute-start | bytes 92168 | tf_op jit(solution)/shard_map/ppermute | solution.py:17
  160.5 4.3 collective-permute-start.15
  163.5 3.1 collective-permute-start.16
  166.8 15.4 %collective-permute-start.17 = (f32[3,8,34,1]{3,1,2,0:T(8,128)S(1)}, f32[3,8,34,1]{3,1,2,0:T(8,128)S(1)}, u32[]{:S(2)}, u32[]{:S(2)}) collective-permute-start(f32[3,8,34,1]{3,1,2,0:T(8,128)S(1)} %get-tuple-element.517), channel_id=1, source_target_pairs={{0,1},{1,2},{2,3},{3,4},{4,5},{5,6},{6,7},{7,8},{8,9},{9,10},{10,1... | collective-permute-start | bytes 9800 | tf_op jit(solution)/shard_map/ppermute | solution.py:27
  169.4 14.6 %collective-permute-start.18 = (f32[3,8,34,1]{3,1,2,0:T(8,128)S(1)}, f32[3,8,34,1]{3,1,2,0:T(8,128)S(1)}, u32[]{:S(2)}, u32[]{:S(2)}) collective-permute-start(f32[3,8,34,1]{3,1,2,0:T(8,128)S(1)} %get-tuple-element.518), channel_id=1, source_target_pairs={{1,0},{2,1},{3,2},{4,3},{5,4},{6,5},{7,6},{8,7},{9,8},{10,9},{11,1... | collective-permute-start | bytes 9800 | tf_op jit(solution)/shard_map/ppermute | solution.py:28
  174.9 9.5 %collective-permute-start.19 = (f32[3,8,320]{2,1,0:T(8,128)S(1)}, f32[3,8,320]{2,1,0:T(8,128)S(1)}, u32[]{:S(2)}, u32[]{:S(2)}) collective-permute-start(f32[3,8,320]{2,1,0:T(8,128)S(1)} %pad_maximum_fusion.22), channel_id=1, source_target_pairs={{0,128},{128,0},{1,129},{129,1},{2,130},{130,2},{3,131},{131,3},{4... | collective-permute-start | bytes 92168 | tf_op jit(solution)/shard_map/ppermute | solution.py:17
  213.8 4.3 collective-permute-start.20
  216.8 3.1 collective-permute-start.21
  220.1 15.4 %collective-permute-start.22 = (f32[3,8,34,1]{3,1,2,0:T(8,128)S(1)}, f32[3,8,34,1]{3,1,2,0:T(8,128)S(1)}, u32[]{:S(2)}, u32[]{:S(2)}) collective-permute-start(f32[3,8,34,1]{3,1,2,0:T(8,128)S(1)} %get-tuple-element.515), channel_id=1, source_target_pairs={{0,1},{1,2},{2,3},{3,4},{4,5},{5,6},{6,7},{7,8},{8,9},{9,10},{10,1... | collective-permute-start | bytes 9800 | tf_op jit(solution)/shard_map/ppermute | solution.py:27
  222.6 14.7 %collective-permute-start.23 = (f32[3,8,34,1]{3,1,2,0:T(8,128)S(1)}, f32[3,8,34,1]{3,1,2,0:T(8,128)S(1)}, u32[]{:S(2)}, u32[]{:S(2)}) collective-permute-start(f32[3,8,34,1]{3,1,2,0:T(8,128)S(1)} %get-tuple-element.516), channel_id=1, source_target_pairs={{1,0},{2,1},{3,2},{4,3},{5,4},{6,5},{7,6},{8,7},{9,8},{10,9},{11,1... | collective-permute-start | bytes 9800 | tf_op jit(solution)/shard_map/ppermute | solution.py:28
  228.3 9.5 %collective-permute-start.24 = (f32[3,8,320]{2,1,0:T(8,128)S(1)}, f32[3,8,320]{2,1,0:T(8,128)S(1)}, u32[]{:S(2)}, u32[]{:S(2)}) collective-permute-start(f32[3,8,320]{2,1,0:T(8,128)S(1)} %pad_maximum_fusion.23), channel_id=1, source_target_pairs={{0,128},{128,0},{1,129},{129,1},{2,130},{130,2},{3,131},{131,3},{4... | collective-permute-start | bytes 92168 | tf_op jit(solution)/shard_map/ppermute | solution.py:17
  267.0 4.3 collective-permute-start.25
  270.0 3.1 collective-permute-start.26
  273.3 15.4 %collective-permute-start.27 = (f32[3,8,34,1]{3,1,2,0:T(8,128)S(1)}, f32[3,8,34,1]{3,1,2,0:T(8,128)S(1)}, u32[]{:S(2)}, u32[]{:S(2)}) collective-permute-start(f32[3,8,34,1]{3,1,2,0:T(8,128)S(1)} %get-tuple-element.513), channel_id=1, source_target_pairs={{0,1},{1,2},{2,3},{3,4},{4,5},{5,6},{6,7},{7,8},{8,9},{9,10},{10,1... | collective-permute-start | bytes 9800 | tf_op jit(solution)/shard_map/ppermute | solution.py:27
  275.2 15.2 %collective-permute-start.28 = (f32[3,8,34,1]{3,1,2,0:T(8,128)S(1)}, f32[3,8,34,1]{3,1,2,0:T(8,128)S(1)}, u32[]{:S(2)}, u32[]{:S(2)}) collective-permute-start(f32[3,8,34,1]{3,1,2,0:T(8,128)S(1)} %get-tuple-element.514), channel_id=1, source_target_pairs={{1,0},{2,1},{3,2},{4,3},{5,4},{6,5},{7,6},{8,7},{9,8},{10,9},{11,1... | collective-permute-start | bytes 9800 | tf_op jit(solution)/shard_map/ppermute | solution.py:28
  281.4 9.5 %collective-permute-start.29 = (f32[3,8,320]{2,1,0:T(8,128)S(1)}, f32[3,8,320]{2,1,0:T(8,128)S(1)}, u32[]{:S(2)}, u32[]{:S(2)}) collective-permute-start(f32[3,8,320]{2,1,0:T(8,128)S(1)} %pad_maximum_fusion.24), channel_id=1, source_target_pairs={{0,128},{128,0},{1,129},{129,1},{2,130},{130,2},{3,131},{131,3},{4... | collective-permute-start | bytes 92168 | tf_op jit(solution)/shard_map/ppermute | solution.py:17
  320.3 4.3 collective-permute-start.30
  323.3 3.1 collective-permute-start.31
  326.6 15.4 %collective-permute-start.32 = (f32[3,8,34,1]{3,1,2,0:T(8,128)S(1)}, f32[3,8,34,1]{3,1,2,0:T(8,128)S(1)}, u32[]{:S(2)}, u32[]{:S(2)}) collective-permute-start(f32[3,8,34,1]{3,1,2,0:T(8,128)S(1)} %get-tuple-element.511), channel_id=1, source_target_pairs={{0,1},{1,2},{2,3},{3,4},{4,5},{5,6},{6,7},{7,8},{8,9},{9,10},{10,1... | collective-permute-start | bytes 9800 | tf_op jit(solution)/shard_map/ppermute | solution.py:27
  328.5 15.2 %collective-permute-start.33 = (f32[3,8,34,1]{3,1,2,0:T(8,128)S(1)}, f32[3,8,34,1]{3,1,2,0:T(8,128)S(1)}, u32[]{:S(2)}, u32[]{:S(2)}) collective-permute-start(f32[3,8,34,1]{3,1,2,0:T(8,128)S(1)} %get-tuple-element.512), channel_id=1, source_target_pairs={{1,0},{2,1},{3,2},{4,3},{5,4},{6,5},{7,6},{8,7},{9,8},{10,9},{11,1... | collective-permute-start | bytes 9800 | tf_op jit(solution)/shard_map/ppermute | solution.py:28
  334.8 9.5 %collective-permute-start.34 = (f32[3,8,320]{2,1,0:T(8,128)S(1)}, f32[3,8,320]{2,1,0:T(8,128)S(1)}, u32[]{:S(2)}, u32[]{:S(2)}) collective-permute-start(f32[3,8,320]{2,1,0:T(8,128)S(1)} %pad_maximum_fusion.25), channel_id=1, source_target_pairs={{0,128},{128,0},{1,129},{129,1},{2,130},{130,2},{3,131},{131,3},{4... | collective-permute-start | bytes 92168 | tf_op jit(solution)/shard_map/ppermute | solution.py:17
  373.6 4.3 collective-permute-start.35
  376.6 3.1 collective-permute-start.36
  379.9 15.4 %collective-permute-start.37 = (f32[3,8,34,1]{3,1,2,0:T(8,128)S(1)}, f32[3,8,34,1]{3,1,2,0:T(8,128)S(1)}, u32[]{:S(2)}, u32[]{:S(2)}) collective-permute-start(f32[3,8,34,1]{3,1,2,0:T(8,128)S(1)} %get-tuple-element.509), channel_id=1, source_target_pairs={{0,1},{1,2},{2,3},{3,4},{4,5},{5,6},{6,7},{7,8},{8,9},{9,10},{10,1... | collective-permute-start | bytes 9800 | tf_op jit(solution)/shard_map/ppermute | solution.py:27
  381.8 15.2 %collective-permute-start.38 = (f32[3,8,34,1]{3,1,2,0:T(8,128)S(1)}, f32[3,8,34,1]{3,1,2,0:T(8,128)S(1)}, u32[]{:S(2)}, u32[]{:S(2)}) collective-permute-start(f32[3,8,34,1]{3,1,2,0:T(8,128)S(1)} %get-tuple-element.510), channel_id=1, source_target_pairs={{1,0},{2,1},{3,2},{4,3},{5,4},{6,5},{7,6},{8,7},{9,8},{10,9},{11,1... | collective-permute-start | bytes 9800 | tf_op jit(solution)/shard_map/ppermute | solution.py:28
  388.1 9.5 %collective-permute-start.39 = (f32[3,8,320]{2,1,0:T(8,128)S(1)}, f32[3,8,320]{2,1,0:T(8,128)S(1)}, u32[]{:S(2)}, u32[]{:S(2)}) collective-permute-start(f32[3,8,320]{2,1,0:T(8,128)S(1)} %pad_maximum_fusion.26), channel_id=1, source_target_pairs={{0,128},{128,0},{1,129},{129,1},{2,130},{130,2},{3,131},{131,3},{4... | collective-permute-start | bytes 92168 | tf_op jit(solution)/shard_map/ppermute | solution.py:17
  426.9 4.3 collective-permute-start.40
  429.9 3.1 collective-permute-start.41
  433.2 15.4 %collective-permute-start.42 = (f32[3,8,34,1]{3,1,2,0:T(8,128)S(1)}, f32[3,8,34,1]{3,1,2,0:T(8,128)S(1)}, u32[]{:S(2)}, u32[]{:S(2)}) collective-permute-start(f32[3,8,34,1]{3,1,2,0:T(8,128)S(1)} %get-tuple-element.507), channel_id=1, source_target_pairs={{0,1},{1,2},{2,3},{3,4},{4,5},{5,6},{6,7},{7,8},{8,9},{9,10},{10,1... | collective-permute-start | bytes 9800 | tf_op jit(solution)/shard_map/ppermute | solution.py:27
  435.2 15.2 %collective-permute-start.43 = (f32[3,8,34,1]{3,1,2,0:T(8,128)S(1)}, f32[3,8,34,1]{3,1,2,0:T(8,128)S(1)}, u32[]{:S(2)}, u32[]{:S(2)}) collective-permute-start(f32[3,8,34,1]{3,1,2,0:T(8,128)S(1)} %get-tuple-element.508), channel_id=1, source_target_pairs={{1,0},{2,1},{3,2},{4,3},{5,4},{6,5},{7,6},{8,7},{9,8},{10,9},{11,1... | collective-permute-start | bytes 9800 | tf_op jit(solution)/shard_map/ppermute | solution.py:28
  441.4 9.5 %collective-permute-start.44 = (f32[3,8,320]{2,1,0:T(8,128)S(1)}, f32[3,8,320]{2,1,0:T(8,128)S(1)}, u32[]{:S(2)}, u32[]{:S(2)}) collective-permute-start(f32[3,8,320]{2,1,0:T(8,128)S(1)} %pad_maximum_fusion.27), channel_id=1, source_target_pairs={{0,128},{128,0},{1,129},{129,1},{2,130},{130,2},{3,131},{131,3},{4... | collective-permute-start | bytes 92168 | tf_op jit(solution)/shard_map/ppermute | solution.py:17
  (3 other events, 46.9 us)
where the time goes:
time: 478 us; the launch traced here: 471 us
  local copies, waits for them, and re-layouts  252 us (53%)
  starting transfers between devices  132 us (28%)
  waiting for transfers between devices  70.7 us (15%)
  other arithmetic  13.4 us (3%)
    scatter x8, local copies, waits for them, and re-layouts, fill_thin(): framed_array.at[:, :, 1:patch_height + 1, patch_breadth + 1]  79.1 us
    ppermute x18, starting transfers between devices, with_halo(): after = lax.ppermute(first, axis, down)  66.6 us
    ppermute x18, starting transfers between devices, with_halo(): before = lax.ppermute(last, axis, up)  46.3 us
    ppermute x18, waiting for transfers between devices, with_halo(): before = lax.ppermute(last, axis, up)  44.4 us
    reshape x7, local copies, waits for them, and re-layouts, on_device(): flow_array.reshape(3, depth_count, -1)  40.1 us
    gather x16, local copies, waits for them, and re-layouts, on_device(): jnp.take(flow_array.reshape(3, depth_count, -1), inner_index, axis=2)  37.8 us
    scatter x8, local copies, waits for them, and re-layouts, fill_thin(): framed_array.at[:, :, 1:patch_height + 1, 0]  28.7 us
    ppermute x18, waiting for transfers between devices, with_halo(): after = lax.ppermute(first, axis, down)  26.3 us
  transfers between devices with their start and end apart: 45, of which 23 were waited for; matrix products, arithmetic and copies ran while one was open for 6% of the time, Pallas kernels for 0%

commit v1 on v0

v1 whole, which is shorter than its diff:
```python
import jax
import jax.numpy as jnp
from jax import lax
from jax.experimental import pallas as pl
from jax.experimental.pallas import tpu as pltpu
from jax.sharding import PartitionSpec as P

ITERS = 8
TIME_STEP = 0.1
BUOYANCY_FACTOR = 10.0
DRAG_COEF = 1.0
MESH = pl.DeviceIdType.MESH
LEVELS, ROWS, COLS = 8, 32, 128


def lane_take(value, index):
    return jnp.take_along_axis(value, index, axis=1, mode="promise_in_bounds")


def kernel(
    n_colat, n_lon,
    heat_in, flow_in, stiff_in, site_in, phase_in,
    heat_out, flow_out,
    flow, source, send_ns, send_we, halo_ns, halo_we, send_sem, recv_sem,
):
    p, c, l = (lax.axis_index(a) for a in ("panel", "colat", "lon"))
    lane = lax.broadcasted_iota(jnp.int32, (LEVELS, COLS), 1)
    level = lax.broadcasted_iota(jnp.int32, (LEVELS, COLS), 0)
    north, south = (c == 0).astype(jnp.int32), (c == n_colat - 1).astype(jnp.int32)
    west, east = (l == 0).astype(jnp.int32), (l == n_lon - 1).astype(jnp.int32)
    other = 1 - p

    def across(edge):
        return p + edge * (other - p)

    sides = (
        ((across(north), c - 1 + north, l), 1 - north),
        ((across(south), c + 1 - south, l), south),
        ((across(west), c, l - 1 + west), 3 - west),
        ((across(east), c, l + 1 - east), 2 + east),
    )
    barrier = pltpu.get_barrier_semaphore()
    for device, _ in sides:
        pl.semaphore_signal(barrier, inc=1, device_id=device, device_id_type=MESH)

    stiff = jnp.zeros((LEVELS, COLS), jnp.float32)
    for k in range(LEVELS):
        stiff = jnp.where(level == k, stiff_in[k], stiff)
    upper = jnp.where(level < LEVELS - 1, 0.5 * (stiff + pltpu.roll(stiff, LEVELS - 1, 0)), 0.0)
    lower = jnp.where(level > 0, 0.5 * (stiff + pltpu.roll(stiff, 1, 0)), 0.0)
    inverse = 1.0 / (DRAG_COEF + 4.0 * stiff + upper + lower)
    coef, above_coef, below_coef = stiff * inverse, upper * inverse, lower * inverse
    buoyancy = BUOYANCY_FACTOR * inverse

    row_of_lane, part_of_lane = lane & (ROWS - 1), lane >> 5

    def sites(j):
        return jnp.broadcast_to(site_in[0, 0:1, COLS * j : COLS * (j + 1)], (LEVELS, COLS))

    def pick(flag, yes, no):
        return jnp.where(flag == 1, yes, no)

    ns_site = pick(north, sites(1), sites(2))
    ns_heat = (pick(north, sites(0), sites(2)), pick(north, sites(1), sites(3)))
    we_site = lane_take(sites(4), pick(west, 2 * row_of_lane + 1, 2 * ROWS + 2 * row_of_lane))
    we_heat = lane_take(
        sites(4), (pick(west, 0, 2 * ROWS) + 2 * row_of_lane + (part_of_lane & 1))
    )
    ns_angle = jnp.broadcast_to(
        pick(north, phase_in[0, 0:1, 0:COLS], phase_in[0, 0:1, COLS : 2 * COLS]), (LEVELS, COLS)
    )
    tail = phase_in[0, 0:1, 2 * COLS : 2 * COLS + 2 * ROWS]
    tail = jnp.broadcast_to(jnp.concatenate([tail, tail], axis=1), (LEVELS, COLS))
    we_angle = lane_take(tail, pick(west, row_of_lane, ROWS + row_of_lane))
    ns_cos, ns_sin = jnp.cos(ns_angle), jnp.sin(ns_angle)
    we_cos, we_sin = jnp.cos(we_angle), jnp.sin(we_angle)

    def heat_row(r):
        return heat_in[pl.ds(r, LEVELS, stride=ROWS), :]

    def collect(index, rows, count):
        at_row, at_col = index >> 7, index & (COLS - 1)
        found = [jnp.zeros((LEVELS, COLS), jnp.float32)] * count
        for r in range(ROWS):
            here = at_row == r
            found = [jnp.where(here, lane_take(rows(r, i), at_col), f) for i, f in enumerate(found)]
        return found

    def flow_row(r, i):
        return flow[r, i]

    def rotated(index, cos, sin):
        a, b, d = collect(index, flow_row, 3)
        return a, cos * b + sin * d, cos * d - sin * b

    def pack(packed, value, t, at):
        return jnp.where(lane == t, pltpu.roll(value, (t - at) % COLS, 1), packed)

    def copies(k, first):
        for side, (device, facing) in enumerate(sides):
            ns = side < 2
            buf, halo = (send_ns, halo_ns) if ns else (send_we, halo_we)
            own, theirs = (side, facing) if ns else (side - 2, facing - 2)
            n = (5 if first else 3) if ns else (2 if first else 1)
            yield pltpu.make_async_remote_copy(
                src_ref=buf.at[k, own, 0:n],
                dst_ref=halo.at[k, theirs, 0:n],
                send_sem=send_sem.at[k, side],
                recv_sem=recv_sem.at[k, facing],
                device_id=device,
                device_id_type=MESH,
            )

    def arrivals(k, first):
        for side, (device, _) in enumerate(sides):
            ns = side < 2
            buf, halo = (send_ns, halo_ns) if ns else (send_we, halo_we)
            own = side if ns else side - 2
            n = (5 if first else 3) if ns else (2 if first else 1)
            yield pltpu.make_async_remote_copy(
                src_ref=buf.at[k, own, 0:n],
                dst_ref=halo.at[k, own, 0:n],
                send_sem=send_sem.at[k, side],
                recv_sem=recv_sem.at[k, side],
                device_id=device,
                device_id_type=MESH,
            )

    def fill_sends(k, packed_west, packed_east):
        for i in range(3):
            send_ns[k, 0, i] = flow[0, i]
            send_ns[k, 1, i] = flow[ROWS - 1, i]
        send_we[k, 0, 0] = packed_west
        send_we[k, 1, 0] = packed_east

        @pl.when((north == 1) | (south == 1))
        def _():
            for i, v in enumerate(rotated(ns_site, ns_cos, ns_sin)):
                send_ns[k, south, i] = v

        @pl.when((west == 1) | (east == 1))
        def _():
            a, b, d = rotated(we_site, we_cos, we_sin)
            send_we[k, east, 0] = jnp.where(
                part_of_lane == 0, a, jnp.where(part_of_lane == 1, b, d)
            )

    zero = jnp.zeros((LEVELS, COLS), jnp.float32)
    packed_west, packed_east, heat_west, heat_east = zero, zero, zero, zero
    for r in range(ROWS):
        for i in range(3):
            value = flow_in[pl.ds(i * LEVELS * ROWS + r, LEVELS, stride=ROWS), :]
            flow[r, i] = value
            packed_west = pack(packed_west, value, i * ROWS + r, 0)
            packed_east = pack(packed_east, value, i * ROWS + r, COLS - 1)
        value = heat_row(r)
        for j in range(2):
            heat_west = pack(heat_west, value, j * ROWS + r, j)
            heat_east = pack(heat_east, value, j * ROWS + r, COLS - 2 + j)
    for j in range(2):
        send_ns[0, 0, 3 + j] = heat_row(j)
        send_ns[0, 1, 3 + j] = heat_row(ROWS - 2 + j)
    send_we[0, 0, 1] = heat_west
    send_we[0, 1, 1] = heat_east
    fill_sends(0, packed_west, packed_east)

    @pl.when((north == 1) | (south == 1))
    def _():
        for j in range(2):
            send_ns[0, south, 3 + j] = collect(ns_heat[j], lambda r, _: heat_row(r), 1)[0]

    @pl.when((west == 1) | (east == 1))
    def _():
        send_we[0, east, 1] = collect(we_heat, lambda r, _: heat_row(r), 1)[0]

    pl.semaphore_wait(barrier, 4)
    for copy in copies(0, True):
        copy.start()
    for copy in arrivals(0, True):
        copy.wait_recv()

    def wide_row(r):
        if r < 0:
            return halo_ns[0, 0, 5 + r]
        if r >= ROWS:
            return halo_ns[0, 1, 3 + r - ROWS]
        return heat_row(r)

    def put(value, packed, t, at):
        return jnp.where(lane == at, pltpu.roll(packed, (at - t) % COLS, 1), value)

    from_west, from_east = halo_we[0, 0, 1], halo_we[0, 1, 1]
    window = [wide_row(r) for r in range(-2, 2)]
    for r in range(ROWS):
        window.append(wide_row(r + 2))
        up2, up1, here, down1, down2 = window[r : r + 5]
        west1 = put(pltpu.roll(here, 1, 1), from_west, ROWS + r, 0)
        west2 = put(put(pltpu.roll(here, 2, 1), from_west, r, 0), from_west, ROWS + r, 1)
        east1 = put(pltpu.roll(here, COLS - 1, 1), from_east, r, COLS - 1)
        east2 = put(
            put(pltpu.roll(here, COLS - 2, 1), from_east, r, COLS - 2), from_east, ROWS + r, COLS - 1
        )
        above = jnp.where(level == LEVELS - 1, here, pltpu.roll(here, LEVELS - 1, 0))
        below = jnp.where(level == 0, here, pltpu.roll(here, 1, 0))
        grad_colat = (8.0 * (down1 - up1) - (down2 - up2)) * (1.0 / 12.0)
        grad_lon = (8.0 * (east1 - west1) - (east2 - west2)) * (1.0 / 12.0)
        grad_rad = (above - below) * 0.5
        laplace = down1 + up1 + east1 + west1 + above + below - 6.0 * here
        advect = flow[r, 0] * grad_rad + flow[r, 1] * grad_colat + flow[r, 2] * grad_lon
        stepped = here + TIME_STEP * (laplace - advect)
        heat_out[pl.ds(r, LEVELS, stride=ROWS), :] = stepped
        source[r] = buoyancy * stepped

    def relax(k, store):
        from_west, from_east = halo_we[k, 0, 0], halo_we[k, 1, 0]
        before = [halo_ns[k, 0, i] for i in range(3)]
        now = [flow[0, i] for i in range(3)]
        for r in range(ROWS):
            after = [halo_ns[k, 1, i] if r == ROWS - 1 else flow[r + 1, i] for i in range(3)]
            for i in range(3):
                t = i * ROWS + r
                here = now[i]
                near = (
                    before[i]
                    + after[i]
                    + put(pltpu.roll(here, 1, 1), from_west, t, 0)
                    + put(pltpu.roll(here, COLS - 1, 1), from_east, t, COLS - 1)
                )
                value = (
                    coef * near
                    + above_coef * pltpu.roll(here, LEVELS - 1, 0)
                    + below_coef * pltpu.roll(here, 1, 0)
                )
                if i == 0:
                    value = value + source[r]
                store(r, i, value)
            before, now = now, after

    def sweep(k, carry):
        packed = [zero, zero]

        def keep(r, i, value):
            flow[r, i] = value
            packed[0] = pack(packed[0], value, i * ROWS + r, 0)
            packed[1] = pack(packed[1], value, i * ROWS + r, COLS - 1)

        relax(k, keep)
        fill_sends(k + 1, *packed)
        for copy in copies(k + 1, False):
            copy.start()
        for copy in arrivals(k + 1, False):
            copy.wait_recv()
        return carry

    lax.fori_loop(0, ITERS - 1, sweep, 0)

    def finish(r, i, value):
        flow_out[pl.ds(i * LEVELS * ROWS + r, LEVELS, stride=ROWS), :] = value

    relax(ITERS - 1, finish)
    for k in range(ITERS):
        for copy in copies(k, k == 0):
            copy.wait_send()


def solution(mesh):
    n_colat, n_lon = mesh.shape["colat"], mesh.shape["lon"]

    def on_device(heat, flow, stiffness, site, phase):
        vmem = pl.BlockSpec(memory_space=pltpu.VMEM)
        block = (LEVELS, COLS)
        heat_out, flow_out = pl.pallas_call(
            lambda *refs: kernel(n_colat, n_lon, *refs),
            out_shape=(
                jax.ShapeDtypeStruct((LEVELS * ROWS, COLS), jnp.float32),
                jax.ShapeDtypeStruct((3 * LEVELS * ROWS, COLS), jnp.float32),
            ),
            in_specs=[vmem, vmem, pl.BlockSpec(memory_space=pltpu.SMEM), vmem, vmem],
            out_specs=(vmem, vmem),
            scratch_shapes=[
                pltpu.VMEM((ROWS, 3, *block), jnp.float32),
                pltpu.VMEM((ROWS, *block), jnp.float32),
                pltpu.VMEM((ITERS, 2, 5, *block), jnp.float32),
                pltpu.VMEM((ITERS, 2, 2, *block), jnp.float32),
                pltpu.VMEM((ITERS, 2, 5, *block), jnp.float32),
                pltpu.VMEM((ITERS, 2, 2, *block), jnp.float32),
                pltpu.SemaphoreType.DMA((ITERS, 4)),
                pltpu.SemaphoreType.DMA((ITERS, 4)),
            ],
            compiler_params=pltpu.CompilerParams(collective_id=0, has_side_effects=True),
            name="mantle_step",
        )(
            heat.reshape(LEVELS * ROWS, COLS),
            flow.reshape(3 * LEVELS * ROWS, COLS),
            stiffness,
            site,
            phase,
        )
        return heat_out.reshape(heat.shape), flow_out.reshape(flow.shape)

    return jax.shard_map(
        on_device,
        mesh=mesh,
        in_specs=(
            P("panel", None, "colat", "lon"),
            P("panel", None, None, "colat", "lon"),
            P(),
            P("panel", "colat", "lon"),
            P("panel", "colat", "lon"),
        ),
        out_specs=(P("panel", None, "colat", "lon"), P("panel", None, None, "colat", "lon")),
        check_vma=False,
    )
```

time: 478 us -> 84.3 us (0.18); the launches traced: 471 us -> 84.1 us
  local copies, waits for them, and re-layouts: 252 us -> 3.33 us
  starting transfers between devices: 132 us -> 0 us
  Pallas kernels: 0 us -> 80.2 us
  waiting for transfers between devices: 70.7 us -> 0 us
  other arithmetic: 13.4 us -> 0 us
    scatter x36 -> x0, local copies, waits for them, and re-layouts: 139 us -> none  [the longest x8 79.1 us: fill_thin(): framed_array.at[:, :, 1:patch_height + 1, patch_breadth + 1]]
    ppermute x45 -> x0, starting transfers between devices: 132 us -> none  [the longest x18 66.6 us: with_halo(): after = lax.ppermute(first, axis, down)]
    pallas_call x0 -> x1, Pallas kernels: none -> 80.2 us  [on_device(): pl.pallas_call(lambda *refs: kernel(n_colat, n_lon, *refs), out_shape=(ja...]
    ppermute x45 -> x0, waiting for transfers between devices: 70.7 us -> none  [the longest x18 44.4 us: with_halo(): before = lax.ppermute(last, axis, up)]
    gather x17 -> x0, local copies, waits for them, and re-layouts: 41 us -> none  [the longest x16 37.8 us: on_device(): jnp.take(flow_array.reshape(3, depth_count, -1), inner_index, axis=2)]
    reshape x11 -> x0, local copies, waits for them, and re-layouts: 40.8 us -> none  [the longest x7 40.1 us: on_device(): flow_array.reshape(3, depth_count, -1)]
    slice x89 -> x0, local copies, waits for them, and re-layouts: 10.1 us -> none  [the longest x15 2.87 us: fill_thin(): framed_array[:, :, 1:patch_height + 1, patch_breadth + 1]]
    another operation x20 -> x0, local copies, waits for them, and re-layouts: 8.29 us -> none
  transfers between devices with their start and end apart: 45 -> 0, of which waited for: 23 -> 0; matrix products, arithmetic and copies ran while one was open for 6% -> 0% of each run, Pallas kernels for 0% -> 0%
where the time goes in v1:
time: 84.3 us; the launch traced here: 84.1 us
  Pallas kernels  80.2 us (95%)
  local copies, waits for them, and re-layouts  3.33 us (4%)
    pallas_call x1, Pallas kernels, on_device(): pl.pallas_call(lambda *refs: kernel(n_colat, n_lon, *refs), out_shape=(ja...  80.2 us
    unnamed x2, local copies, waits for them, and re-layouts  3.33 us

profile of v1, /device:TPU:6, one launch (start us, length us, event | category | flops | bytes accessed | tf_op | source)
XLA Modules:
  0.0 84.1 jit_solution(10494423310447350910)
XLA Ops:
  0.6 80.2 %mantle_step.1 = (f32[256,128]{1,0:T(8,128)}, f32[768,128]{1,0:T(8,128)}) custom-call(f32[256,128]{1,0:T(8,128)} %bitcast.6, f32[768,128]{1,0:T(8,128)} %bitcast.4, f32[8]{0:T(128)} %refs_2_.1, s32[1,1,640]{2,1,0:T(1,128)} %refs_3_.1, f32[1,1,320]{2,1,0:T(1,128)} %refs_4_.1), custom_call_target="tpu_custom_call" | custom-call | tf_op jit(solution)/shard_map/mantle_step/pallas_call | solution.py:272
  80.8 1.6 %copy.9 = f32[1,8,32,128]{3,2,1,0:T(8,128)} copy(f32[1,8,32,128]{3,2,1,0:T(8,128)} %bitcast.7) | data formatting | bytes 262144
  82.4 1.8 %copy.10 = f32[1,3,8,32,128]{4,3,2,1,0:T(8,128)} copy(f32[1,3,8,32,128]{4,3,2,1,0:T(8,128)} %bitcast.5) | data formatting | bytes 786432

commit v2 on v1

v2 whole, which is shorter than its diff:
```python
import jax
import jax.numpy as jnp
from jax import lax
from jax.experimental import pallas as pl
from jax.experimental.pallas import tpu as pltpu
from jax.sharding import PartitionSpec as P

ITERS = 8
TIME_STEP = 0.1
BUOYANCY_FACTOR = 10.0
DRAG_COEF = 1.0
MESH = pl.DeviceIdType.MESH
LEVELS, ROWS, COLS = 8, 32, 128


def lane_take(value, index):
    return jnp.take_along_axis(value, index, axis=1, mode="promise_in_bounds")


def kernel(
    n_colat, n_lon,
    heat_in, flow_in, stiff_in, site_in, phase_in,
    heat_out, flow_out,
    flow, source, found, send_ns, send_we, halo_ns, halo_we, send_sem, recv_sem,
):
    p, c, l = (lax.axis_index(a) for a in ("panel", "colat", "lon"))
    lane = lax.broadcasted_iota(jnp.int32, (LEVELS, COLS), 1)
    level = lax.broadcasted_iota(jnp.int32, (LEVELS, COLS), 0)
    north, south = (c == 0).astype(jnp.int32), (c == n_colat - 1).astype(jnp.int32)
    west, east = (l == 0).astype(jnp.int32), (l == n_lon - 1).astype(jnp.int32)
    at_rim = (north, south, west, east)

    def across(edge):
        return p + edge * (1 - 2 * p)

    sides = (
        ((across(north), c - 1 + north, l), 1 - north),
        ((across(south), c + 1 - south, l), south),
        ((across(west), c, l - 1 + west), 3 - west),
        ((across(east), c, l + 1 - east), 2 + east),
    )
    barrier = pltpu.get_barrier_semaphore()
    for device, _ in sides:
        pl.semaphore_signal(barrier, inc=1, device_id=device, device_id_type=MESH)

    stiff = jnp.zeros((LEVELS, COLS), jnp.float32)
    for k in range(LEVELS):
        stiff = jnp.where(level == k, stiff_in[k], stiff)
    upper = jnp.where(level < LEVELS - 1, 0.5 * (stiff + pltpu.roll(stiff, LEVELS - 1, 0)), 0.0)
    lower = jnp.where(level > 0, 0.5 * (stiff + pltpu.roll(stiff, 1, 0)), 0.0)
    inverse = 1.0 / (DRAG_COEF + 4.0 * stiff + upper + lower)
    coef, above_coef, below_coef = stiff * inverse, upper * inverse, lower * inverse
    buoyancy = BUOYANCY_FACTOR * inverse

    zero = jnp.zeros((LEVELS, COLS), jnp.float32)
    is_even = (lane & 1) == 0
    on_edge = (lane == 0) | (lane == COLS - 1)

    def shift(value, by):
        return pltpu.roll(value, by % COLS, 1)

    def pick(flag, yes, no):
        return jnp.where(flag == 1, yes, no)

    slot = (lane + west) & (COLS - 1)
    slot_row, slot_part = slot & (ROWS - 1), slot >> 5
    heat_slot = (lane + 2 * west) & (COLS - 1)

    def sites(j):
        return jnp.broadcast_to(site_in[0, 0:1, COLS * j : COLS * (j + 1)], (LEVELS, COLS))

    ns_site = pick(north, sites(1), sites(2))
    ns_heat = (pick(north, sites(0), sites(2)), pick(north, sites(1), sites(3)))
    we_base = pick(west, 0, 2 * ROWS)
    we_site = lane_take(sites(4), we_base + west + 2 * slot_row)
    we_heat = lane_take(sites(4), we_base + 2 * (heat_slot >> 2) + (heat_slot & 1))
    ns_angle = jnp.broadcast_to(
        pick(north, phase_in[0, 0:1, 0:COLS], phase_in[0, 0:1, COLS : 2 * COLS]), (LEVELS, COLS)
    )
    tail = phase_in[0, 0:1, 2 * COLS : 2 * COLS + 2 * ROWS]
    tail = jnp.broadcast_to(jnp.concatenate([tail, tail], axis=1), (LEVELS, COLS))
    we_angle = lane_take(tail, pick(west, 0, ROWS) + slot_row)

    def heat_row(r):
        return heat_in[pl.ds(r, LEVELS, stride=ROWS), :]

    def collect(index, rows, count):
        at_row, at_col = index >> 7, index & (COLS - 1)
        values = [zero] * count
        for r in range(ROWS):
            here = at_row == r
            values = [
                jnp.where(here, lane_take(rows(r, i), at_col), v) for i, v in enumerate(values)
            ]
        return values

    def flow_row(r, i):
        return flow[r, i]

    def copy(k, par, first, side, arriving=False):
        device, facing = sides[side]
        ns = side < 2
        buf, halo = (send_ns, halo_ns) if ns else (send_we, halo_we)
        own, theirs = (side, facing) if ns else (side - 2, facing - 2)
        n = (5 if first else 3) if ns else (2 if first else 1)

        at, seen = (own, side) if arriving else (theirs, facing)
        return pltpu.make_async_remote_copy(
            src_ref=buf.at[k, own, 0:n],
            dst_ref=halo.at[k, at, 0:n],
            send_sem=send_sem.at[par, side],
            recv_sem=recv_sem.at[par, seen],
            device_id=device,
            device_id_type=MESH,
        )

    def on_rim(flag_a, flag_b):
        return pl.when((flag_a == 1) | (flag_b == 1))

    def start(k, par, first, side):
        copy(k, par, first, side).start()

    def wait_all(k, par, first):
        for side in range(4):
            copy(k, par, first, side, arriving=True).wait_recv()

    def wait_sent(k, par, first):
        for side in range(4):
            copy(k, par, first, side).wait_send()

    def pack_all(rows):
        packed = [[zero, zero], [zero, zero]]
        for r in range(ROWS):
            for i in range(3):
                part = shift(jnp.where(on_edge, rows(r, i), 0.0), i * ROWS + r)
                packed[r & 1][(r >> 1) & 1] = packed[r & 1][(r >> 1) & 1] + part
        return packed[0][0] + packed[0][1], packed[1][0] + packed[1][1]

    def find(rows):
        @on_rim(north, south)
        def _():
            for i, v in enumerate(collect(ns_site, rows, 3)):
                found[i] = v

        @on_rim(west, east)
        def _():
            for i, v in enumerate(collect(we_site, rows, 3)):
                found[3 + i] = v

    def rotated(values, angle):
        a, b, d = values
        cos, sin = found[angle], found[angle + 1]
        return a, cos * b + sin * d, cos * d - sin * b

    def send_found(k, par, first, patch):
        @on_rim(north, south)
        def _():
            values = patch([found[i] for i in range(3)], ns_site)
            for i, v in enumerate(rotated(values, 6)):
                send_ns[k, south, i] = v

            @pl.when(north == 1)
            def _():
                start(k, par, first, 0)

            @pl.when(south == 1)
            def _():
                start(k, par, first, 1)

        @on_rim(west, east)
        def _():
            values = patch([found[3 + i] for i in range(3)], we_site)
            a, b, d = rotated(values, 8)
            send_we[k, east, 0] = jnp.where(slot_part == 0, a, jnp.where(slot_part == 1, b, d))

            @pl.when(west == 1)
            def _():
                start(k, par, first, 2)

            @pl.when(east == 1)
            def _():
                start(k, par, first, 3)

    def send_inside(k, par, first):
        for side in (2, 3, 0, 1):

            @pl.when(at_rim[side] == 0)
            def _(side=side):
                start(k, par, first, side)

    def first_row(r, i):
        return flow_in[pl.ds(i * LEVELS * ROWS + r, LEVELS, stride=ROWS), :]

    even, odd = pack_all(first_row)
    near_edge = (lane < 2) | (lane >= COLS - 2)
    heat_packed = [zero, zero]
    for r in range(ROWS):
        part = shift(jnp.where(near_edge, heat_row(r), 0.0), 4 * r)
        heat_packed[r & 1] = heat_packed[r & 1] + part
    heat_packed = heat_packed[0] + heat_packed[1]
    for j in range(2):
        send_ns[0, 0, 3 + j] = heat_row(j)
        send_ns[0, 1, 3 + j] = heat_row(ROWS - 2 + j)
        send_we[0, j, 1] = heat_packed
    for i in range(3):
        send_ns[0, 0, i] = first_row(0, i)
        send_ns[0, 1, i] = first_row(ROWS - 1, i)
    send_we[0, 0, 0] = jnp.where(is_even, even, odd)
    send_we[0, 1, 0] = jnp.where(is_even, odd, even)

    @on_rim(north, south)
    def _():
        found[6], found[7] = jnp.cos(ns_angle), jnp.sin(ns_angle)
        for j in range(2):
            send_ns[0, south, 3 + j] = collect(ns_heat[j], lambda r, _: heat_row(r), 1)[0]

    @on_rim(west, east)
    def _():
        found[8], found[9] = jnp.cos(we_angle), jnp.sin(we_angle)
        send_we[0, east, 1] = collect(we_heat, lambda r, _: heat_row(r), 1)[0]

    find(first_row)
    pl.semaphore_wait(barrier, 4)
    send_inside(0, 0, True)
    send_found(0, 0, True, lambda values, index: values)

    def relax(rows, source=None):
        before = [zero] * 3
        now = [rows(0, i) for i in range(3)]
        for r in range(ROWS):
            after = [rows(r + 1, i) for i in range(3)] if r < ROWS - 1 else [zero] * 3
            for i in range(3):
                here = now[i]
                near = (
                    (before[i] + after[i])
                    + jnp.where(lane == 0, 0.0, shift(here, 1))
                    + jnp.where(lane == COLS - 1, 0.0, shift(here, -1))
                )
                value = (
                    coef * near
                    + above_coef * pltpu.roll(here, LEVELS - 1, 0)
                    + below_coef * pltpu.roll(here, 1, 0)
                )
                if i == 0 and source is not None:
                    value = value + source[r]
                flow[r, i] = value
            before, now = now, after

    def completed(k):
        first_cols, last_cols = halo_we[k, 1, 0], shift(halo_we[k, 0, 0], 2)
        pair = (
            coef * jnp.where(is_even, first_cols, last_cols),
            coef * jnp.where(is_even, last_cols, first_cols),
        )

        def rows(r, i):
            value = flow[r, i] + jnp.where(on_edge, shift(pair[r & 1], COLS - 1 - i * ROWS - r), 0.0)
            if r == 0:
                value = value + coef * halo_ns[k, 0, i]
            if r == ROWS - 1:
                value = value + coef * halo_ns[k, 1, i]
            return value

        return rows

    def send_edges(k, par, even, odd):
        above = [coef * halo_ns[k, 0, i] for i in range(3)]
        below = [coef * halo_ns[k, 1, i] for i in range(3)]
        last, first = coef * halo_we[k, 0, 0], coef * halo_we[k, 1, 0]
        for i in range(3):
            even = even + shift(jnp.where(on_edge, above[i], 0.0), i * ROWS)
            odd = odd + shift(jnp.where(on_edge, below[i], 0.0), i * ROWS + ROWS - 1)
        send_we[k + 1, 0, 0] = jnp.where(is_even, even, odd) + shift(last, 1)
        send_we[k + 1, 1, 0] = jnp.where(is_even, odd, even) + shift(first, -1)
        for own, r, halo in ((0, 0, above), (1, ROWS - 1, below)):
            for i in range(3):
                t = i * ROWS + r
                send_ns[k + 1, own, i] = (
                    flow[r, i]
                    + halo[i]
                    + jnp.where(lane == 0, shift(last, 1 - t), 0.0)
                    + jnp.where(lane == COLS - 1, shift(first, COLS - 1 - t), 0.0)
                )
        send_inside(k + 1, par, False)

        def patch(values, index):
            at_row, at_col = index >> 7, index & (COLS - 1)
            for i in range(3):
                slot = i * ROWS + at_row
                add = jnp.where(at_row == 0, lane_take(above[i], at_col), 0.0)
                add = add + jnp.where(at_row == ROWS - 1, lane_take(below[i], at_col), 0.0)
                add = add + jnp.where(at_col == 0, lane_take(last, (slot - 1) & (COLS - 1)), 0.0)
                add = add + jnp.where(at_col == COLS - 1, lane_take(first, slot), 0.0)
                values[i] = values[i] + add
            return values

        send_found(k + 1, par, False, patch)

    relax(first_row)
    wait_all(0, 0, True)

    def wide_row(r):
        if r < 0:
            return halo_ns[0, 0, 5 + r]
        if r >= ROWS:
            return halo_ns[0, 1, 3 + r - ROWS]
        return heat_row(r)

    around = jnp.where((lane & 3) < 2, halo_we[0, 1, 1], halo_we[0, 0, 1])
    window = [wide_row(r) for r in range(-2, 2)]
    for r in range(ROWS):
        window.append(wide_row(r + 2))
        up2, up1, here, down1, down2 = window[r : r + 5]
        rim = shift(around, -4 * r)
        west1 = shift(jnp.where(lane == COLS - 1, rim, here), 1)
        west2 = shift(jnp.where(lane >= COLS - 2, rim, here), 2)
        east1 = shift(jnp.where(lane == 0, rim, here), -1)
        east2 = shift(jnp.where(lane < 2, rim, here), -2)
        above = jnp.where(level == LEVELS - 1, here, pltpu.roll(here, LEVELS - 1, 0))
        below = jnp.where(level == 0, here, pltpu.roll(here, 1, 0))
        grad_colat = (8.0 * (down1 - up1) - (down2 - up2)) * (1.0 / 12.0)
        grad_lon = (8.0 * (east1 - west1) - (east2 - west2)) * (1.0 / 12.0)
        grad_rad = (above - below) * 0.5
        laplace = down1 + up1 + east1 + west1 + above + below - 6.0 * here
        advect = first_row(r, 0) * grad_rad + first_row(r, 1) * grad_colat + first_row(r, 2) * grad_lon
        stepped = here + TIME_STEP * (laplace - advect)
        heat_out[pl.ds(r, LEVELS, stride=ROWS), :] = stepped
        source[r] = buoyancy * stepped
        flow[r, 0] = flow[r, 0] + source[r]

    even, odd = pack_all(flow_row)
    find(flow_row)
    send_edges(0, 1, even, odd)

    def step(k, carry):
        par = k & 1
        relax(completed(k - 1), source)
        even, odd = pack_all(flow_row)
        find(flow_row)
        wait_all(k, par, False)

        @pl.when(k > 1)
        def _():
            wait_sent(k - 1, 1 - par, False)

        send_edges(k, 1 - par, even, odd)
        return carry

    wait_sent(0, 0, True)
    lax.fori_loop(1, ITERS - 1, step, 0)
    relax(completed(ITERS - 2), source)
    last_par = (ITERS - 1) & 1
    wait_all(ITERS - 1, last_par, False)
    rows = completed(ITERS - 1)
    for r in range(ROWS):
        for i in range(3):
            flow_out[pl.ds(i * LEVELS * ROWS + r, LEVELS, stride=ROWS), :] = rows(r, i)
    wait_sent(ITERS - 2, 1 - last_par, False)
    wait_sent(ITERS - 1, last_par, False)


def solution(mesh):
    n_colat, n_lon = mesh.shape["colat"], mesh.shape["lon"]

    def on_device(heat, flow, stiffness, site, phase):
        vmem = pl.BlockSpec(memory_space=pltpu.VMEM)
        block = (LEVELS, COLS)
        heat_out, flow_out = pl.pallas_call(
            lambda *refs: kernel(n_colat, n_lon, *refs),
            out_shape=(
                jax.ShapeDtypeStruct((LEVELS * ROWS, COLS), jnp.float32),
                jax.ShapeDtypeStruct((3 * LEVELS * ROWS, COLS), jnp.float32),
            ),
            in_specs=[vmem, vmem, pl.BlockSpec(memory_space=pltpu.SMEM), vmem, vmem],
            out_specs=(vmem, vmem),
            scratch_shapes=[
                pltpu.VMEM((ROWS, 3, *block), jnp.float32),
                pltpu.VMEM((ROWS, *block), jnp.float32),
                pltpu.VMEM((10, *block), jnp.float32),
                pltpu.VMEM((ITERS, 2, 5, *block), jnp.float32),
                pltpu.VMEM((ITERS, 2, 2, *block), jnp.float32),
                pltpu.VMEM((ITERS, 2, 5, *block), jnp.float32),
                pltpu.VMEM((ITERS, 2, 2, *block), jnp.float32),
                pltpu.SemaphoreType.DMA((2, 4)),
                pltpu.SemaphoreType.DMA((2, 4)),
            ],
            compiler_params=pltpu.CompilerParams(collective_id=0, has_side_effects=True),
            name="mantle_step",
        )(
            heat.reshape(LEVELS * ROWS, COLS),
            flow.reshape(3 * LEVELS * ROWS, COLS),
            stiffness,
            site,
            phase,
        )
        return heat_out.reshape(heat.shape), flow_out.reshape(flow.shape)

    return jax.shard_map(
        on_device,
        mesh=mesh,
        in_specs=(
            P("panel", None, "colat", "lon"),
            P("panel", None, None, "colat", "lon"),
            P(),
            P("panel", "colat", "lon"),
            P("panel", "colat", "lon"),
        ),
        out_specs=(P("panel", None, "colat", "lon"), P("panel", None, None, "colat", "lon")),
        check_vma=False,
    )
```

time: 84.3 us -> 44.5 us (0.53)
  Pallas kernels: 80.2 us -> 40.4 us
    pallas_call x1, Pallas kernels: 80.2 us -> 40.4 us  [on_device(): pl.pallas_call(lambda *refs: kernel(n_colat, n_lon, *refs), out_shape=(ja...]
where the time goes in v2:
time: 44.5 us; the launch traced here: 44.4 us
  Pallas kernels  40.4 us (91%)
  local copies, waits for them, and re-layouts  3.33 us (7%)
  between operations  0.64 us (1%)
    pallas_call x1, Pallas kernels, on_device(): pl.pallas_call(lambda *refs: kernel(n_colat, n_lon, *refs), out_shape=(ja...  40.4 us
    unnamed x2, local copies, waits for them, and re-layouts  3.33 us

profile of v2, /device:TPU:6, one launch (start us, length us, event | category | flops | bytes accessed | tf_op | source)
XLA Modules:
  0.0 44.4 jit_solution(5445857694850367988)
XLA Ops:
  0.6 40.4 %mantle_step.1 = (f32[256,128]{1,0:T(8,128)}, f32[768,128]{1,0:T(8,128)}) custom-call(f32[256,128]{1,0:T(8,128)} %bitcast.6, f32[768,128]{1,0:T(8,128)} %bitcast.4, f32[8]{0:T(128)} %refs_2_.1, s32[1,1,640]{2,1,0:T(1,128)} %refs_3_.1, f32[1,1,320]{2,1,0:T(1,128)} %refs_4_.1), custom_call_target="tpu_custom_call" | custom-call | tf_op jit(solution)/shard_map/mantle_step/pallas_call | solution.py:368
  41.0 1.6 %copy.9 = f32[1,8,32,128]{3,2,1,0:T(8,128)} copy(f32[1,8,32,128]{3,2,1,0:T(8,128)} %bitcast.7) | data formatting | bytes 262144
  42.6 1.8 %copy.10 = f32[1,3,8,32,128]{4,3,2,1,0:T(8,128)} copy(f32[1,3,8,32,128]{4,3,2,1,0:T(8,128)} %bitcast.5) | data formatting | bytes 786432

commit v3 on v2

--- a/solution.py
+++ b/solution.py
@@ -19,8 +19,9 @@
 
 def kernel(
     n_colat, n_lon,
-    heat_in, flow_in, stiff_in, site_in, phase_in,
-    heat_out, flow_out,
+    heat_hbm, flow_hbm, stiff_hbm, site_hbm, phase_hbm,
+    heat_done, flow_done,
+    heat_in, flow_in, stiff_in, site_in, phase_in, heat_out, flow_out, in_sem, out_sem,
     flow, source, found, send_ns, send_we, halo_ns, halo_we, send_sem, recv_sem,
 ):
     p, c, l = (lax.axis_index(a) for a in ("panel", "colat", "lon"))
@@ -42,6 +43,22 @@
     barrier = pltpu.get_barrier_semaphore()
     for device, _ in sides:
         pl.semaphore_signal(barrier, inc=1, device_id=device, device_id_type=MESH)
+    inputs = [
+        pltpu.make_async_copy(src, dst, in_sem.at[n])
+        for n, (src, dst) in enumerate(
+            (
+                (stiff_hbm, stiff_in),
+                (site_hbm, site_in),
+                (phase_hbm, phase_in),
+                (flow_hbm, flow_in),
+                (heat_hbm, heat_in),
+            )
+        )
+    ]
+    for n in (3, 4, 0, 1, 2):
+        inputs[n].start()
+    for n in (0, 1, 2):
+        inputs[n].wait()
 
     stiff = jnp.zeros((LEVELS, COLS), jnp.float32)
     for k in range(LEVELS):
@@ -191,7 +208,17 @@
     def first_row(r, i):
         return flow_in[pl.ds(i * LEVELS * ROWS + r, LEVELS, stride=ROWS), :]
 
+    @on_rim(north, south)
+    def _():
+        found[6], found[7] = jnp.cos(ns_angle), jnp.sin(ns_angle)
+
+    @on_rim(west, east)
+    def _():
+        found[8], found[9] = jnp.cos(we_angle), jnp.sin(we_angle)
+
+    inputs[3].wait()
     even, odd = pack_all(first_row)
+    inputs[4].wait()
     near_edge = (lane < 2) | (lane >= COLS - 2)
     heat_packed = [zero, zero]
     for r in range(ROWS):
@@ -208,20 +235,19 @@
     send_we[0, 0, 0] = jnp.where(is_even, even, odd)
     send_we[0, 1, 0] = jnp.where(is_even, odd, even)
 
+    pl.semaphore_wait(barrier, 4)
+    send_inside(0, 0, True)
+
     @on_rim(north, south)
     def _():
-        found[6], found[7] = jnp.cos(ns_angle), jnp.sin(ns_angle)
         for j in range(2):
             send_ns[0, south, 3 + j] = collect(ns_heat[j], lambda r, _: heat_row(r), 1)[0]
 
     @on_rim(west, east)
     def _():
-        found[8], found[9] = jnp.cos(we_angle), jnp.sin(we_angle)
         send_we[0, east, 1] = collect(we_heat, lambda r, _: heat_row(r), 1)[0]
 
     find(first_row)
-    pl.semaphore_wait(barrier, 4)
-    send_inside(0, 0, True)
     send_found(0, 0, True, lambda values, index: values)
 
     def relax(rows, source=None):
@@ -327,6 +353,8 @@
         heat_out[pl.ds(r, LEVELS, stride=ROWS), :] = stepped
         source[r] = buoyancy * stepped
         flow[r, 0] = flow[r, 0] + source[r]
+    heat_copy = pltpu.make_async_copy(heat_out, heat_done, out_sem.at[3])
+    heat_copy.start()
 
     even, odd = pack_all(flow_row)
     find(flow_row)
@@ -352,46 +380,95 @@
     last_par = (ITERS - 1) & 1
     wait_all(ITERS - 1, last_par, False)
     rows = completed(ITERS - 1)
-    for r in range(ROWS):
-        for i in range(3):
+    results = []
+    for i in range(3):
+        for r in range(ROWS):
             flow_out[pl.ds(i * LEVELS * ROWS + r, LEVELS, stride=ROWS), :] = rows(r, i)
+        span = pl.ds(i * LEVELS * ROWS, LEVELS * ROWS)
+        results.append(pltpu.make_async_copy(flow_out.at[span], flow_done.at[span], out_sem.at[i]))
+        results[-1].start()
     wait_sent(ITERS - 2, 1 - last_par, False)
     wait_sent(ITERS - 1, last_par, False)
+    heat_copy.wait()
+    for result in results:
+        result.wait()
+
+
+def deliver(heat_in, flow_in, heat_out, flow_out, heat, flow, sem):
+    size = LEVELS * ROWS
+    pieces = [(heat_in, heat, heat_out, pl.ds(0, size))]
+    pieces += [(flow_in, flow, flow_out, pl.ds(i * size, size)) for i in range(3)]
+    into = [
+        pltpu.make_async_copy(src.at[span], held.at[span], sem.at[0, n])
+        for n, (src, held, _, span) in enumerate(pieces)
+    ]
+    out = [
+        pltpu.make_async_copy(held.at[span], dst.at[span], sem.at[1, n])
+        for n, (_, held, dst, span) in enumerate(pieces)
+    ]
+    for copy in into:
+        copy.start()
+    for first, second in zip(into, out):
+        first.wait()
+        second.start()
+    for copy in out:
+        copy.wait()
 
 
 def solution(mesh):
     n_colat, n_lon = mesh.shape["colat"], mesh.shape["lon"]
 
+    block = (LEVELS, COLS)
+    heat_shape = jax.ShapeDtypeStruct((LEVELS * ROWS, COLS), jnp.float32)
+    flow_shape = jax.ShapeDtypeStruct((3 * LEVELS * ROWS, COLS), jnp.float32)
+    anywhere = pl.BlockSpec(memory_space=pl.ANY)
+    step = pl.pallas_call(
+        lambda *refs: kernel(n_colat, n_lon, *refs),
+        out_shape=(heat_shape, flow_shape),
+        in_specs=[anywhere] * 5,
+        out_specs=(anywhere, anywhere),
+        scratch_shapes=[
+            pltpu.VMEM(heat_shape.shape, jnp.float32),
+            pltpu.VMEM(flow_shape.shape, jnp.float32),
+            pltpu.SMEM((LEVELS,), jnp.float32),
+            pltpu.VMEM((1, 1, 4 * (COLS + ROWS)), jnp.int32),
+            pltpu.VMEM((1, 1, 2 * (COLS + ROWS)), jnp.float32),
+            pltpu.VMEM(heat_shape.shape, jnp.float32),
+            pltpu.VMEM(flow_shape.shape, jnp.float32),
+            pltpu.SemaphoreType.DMA((5,)),
+            pltpu.SemaphoreType.DMA((4,)),
+            pltpu.VMEM((ROWS, 3, *block), jnp.float32),
+            pltpu.VMEM((ROWS, *block), jnp.float32),
+            pltpu.VMEM((10, *block), jnp.float32),
+            pltpu.VMEM((ITERS, 2, 5, *block), jnp.float32),
+            pltpu.VMEM((ITERS, 2, 2, *block), jnp.float32),
+            pltpu.VMEM((ITERS, 2, 5, *block), jnp.float32),
+            pltpu.VMEM((ITERS, 2, 2, *block), jnp.float32),
+            pltpu.SemaphoreType.DMA((2, 4)),
+            pltpu.SemaphoreType.DMA((2, 4)),
+        ],
+        compiler_params=pltpu.CompilerParams(collective_id=0, has_side_effects=True, vmem_limit_bytes=8 << 20),
+        name="mantle_step",
+    )
+    place = pl.pallas_call(
+        deliver,
+        out_shape=(heat_shape, flow_shape),
+        in_specs=[anywhere] * 2,
+        out_specs=(anywhere, anywhere),
+        scratch_shapes=[
+            pltpu.VMEM(heat_shape.shape, jnp.float32),
+            pltpu.VMEM(flow_shape.shape, jnp.float32),
+            pltpu.SemaphoreType.DMA((2, 4)),
+        ],
+        compiler_params=pltpu.CompilerParams(vmem_limit_bytes=4 << 20),
+        name="deliver",
+    )
+
     def on_device(heat, flow, stiffness, site, phase):
-        vmem = pl.BlockSpec(memory_space=pltpu.VMEM)
-        block = (LEVELS, COLS)
-        heat_out, flow_out = pl.pallas_call(
-            lambda *refs: kernel(n_colat, n_lon, *refs),
-            out_shape=(
-                jax.ShapeDtypeStruct((LEVELS * ROWS, COLS), jnp.float32),
-                jax.ShapeDtypeStruct((3 * LEVELS * ROWS, COLS), jnp.float32),
-            ),
-            in_specs=[vmem, vmem, pl.BlockSpec(memory_space=pltpu.SMEM), vmem, vmem],
-            out_specs=(vmem, vmem),
-            scratch_shapes=[
-                pltpu.VMEM((ROWS, 3, *block), jnp.float32),
-                pltpu.VMEM((ROWS, *block), jnp.float32),
-                pltpu.VMEM((10, *block), jnp.float32),
-                pltpu.VMEM((ITERS, 2, 5, *block), jnp.float32),
-                pltpu.VMEM((ITERS, 2, 2, *block), jnp.float32),
-                pltpu.VMEM((ITERS, 2, 5, *block), jnp.float32),
-                pltpu.VMEM((ITERS, 2, 2, *block), jnp.float32),
-                pltpu.SemaphoreType.DMA((2, 4)),
-                pltpu.SemaphoreType.DMA((2, 4)),
-            ],
-            compiler_params=pltpu.CompilerParams(collective_id=0, has_side_effects=True),
-            name="mantle_step",
-        )(
-            heat.reshape(LEVELS * ROWS, COLS),
-            flow.reshape(3 * LEVELS * ROWS, COLS),
-            stiffness,
-            site,
-            phase,
+        heat_out, flow_out = place(
+            *step(
+                heat.reshape(heat_shape.shape), flow.reshape(flow_shape.shape), stiffness, site, phase
+            )
         )
         return heat_out.reshape(heat.shape), flow_out.reshape(flow.shape)
 

time: 44.5 us -> 45.3 us (1.018)
  Pallas kernels: 40.4 us -> 41.2 us
    pallas_call x1 -> x2, Pallas kernels: 40.4 us -> 41.2 us  [the longest x1 39.6 us: on_device(): step(heat.reshape(heat_shape.shape), flow.reshape(flow_shape.shape), stif...]
    unnamed x2 -> x10, local copies, waits for them, and re-layouts: 3.33 us -> 3.25 us
where the time goes in v3:
time: 45.3 us; the launch traced here: 45.1 us
  Pallas kernels  41.2 us (91%)
  local copies, waits for them, and re-layouts  3.25 us (7%)
  between operations  0.66 us (1%)
    pallas_call x1, Pallas kernels, on_device(): step(heat.reshape(heat_shape.shape), flow.reshape(flow_shape.shape), stif...  39.6 us
    unnamed x10, local copies, waits for them, and re-layouts  3.25 us
    pallas_call x1, Pallas kernels, on_device(): place(*step(heat.reshape(heat_shape.shape), flow.reshape(flow_shape.shape...  1.53 us

profile of v3, /device:TPU:6, one launch (start us, length us, event | category | flops | bytes accessed | tf_op | source)
XLA Modules:
  0.0 45.1 jit_solution(2816888638844703826)
XLA Ops:
  0.6 0.0 copy-start.2
  0.6 0.0 copy-start.4
  0.7 0.7 %copy-done.2 = s32[1,1,640]{2,1,0:T(1,128)S(1)} copy-done((s32[1,1,640]{2,1,0:T(1,128)S(1)}, s32[1,1,640]{2,1,0:T(1,128)}, u32[]{:S(2)}) %copy-start.2) | copy-done | bytes 2584
  1.3 0.0 copy-done.4
  1.3 0.0 copy-start
  1.3 1.0 %copy-done = f32[1,3,8,32,128]{4,3,2,1,0:T(8,128)S(1)} copy-done((f32[1,3,8,32,128]{4,3,2,1,0:T(8,128)S(1)}, f32[1,3,8,32,128]{4,3,2,1,0:T(8,128)}, u32[]{:S(2)}) %copy-start) | copy-done | bytes 393240
  2.3 0.0 copy-start.1
  2.3 0.9 %copy-done.1 = f32[1,8,32,128]{3,2,1,0:T(8,128)S(1)} copy-done((f32[1,8,32,128]{3,2,1,0:T(8,128)S(1)}, f32[1,8,32,128]{3,2,1,0:T(8,128)}, u32[]{:S(2)}) %copy-start.1) | copy-done | bytes 131096
  3.2 0.0 copy-start.3
  3.2 0.7 %copy-done.3 = f32[1,1,320]{2,1,0:T(1,128)S(1)} copy-done((f32[1,1,320]{2,1,0:T(1,128)S(1)}, f32[1,1,320]{2,1,0:T(1,128)}, u32[]{:S(2)}) %copy-start.3) | copy-done | bytes 1304
  3.9 39.6 %mantle_step.1 = (f32[256,128]{1,0:T(8,128)S(1)}, f32[768,128]{1,0:T(8,128)S(1)}) custom-call(f32[256,128]{1,0:T(8,128)S(1)} %bitcast.5, f32[768,128]{1,0:T(8,128)S(1)} %bitcast.4, f32[8]{0:T(128)S(1)} %copy-done.4, s32[1,1,640]{2,1,0:T(1,128)S(1)} %copy-done.2, f32[1,1,320]{2,1,0:T(1,128)S(1)} %copy-done.3), custom_call_target="tpu_custom_call" | custom-call | tf_op jit(solution)/shard_map/mantle_step/pallas_call | solution.py:469
  43.5 1.5 %deliver.1 = (f32[256,128]{1,0:T(8,128)}, f32[768,128]{1,0:T(8,128)}) custom-call(f32[256,128]{1,0:T(8,128)S(1)} %get-tuple-element.6.heat_in, f32[768,128]{1,0:T(8,128)S(1)} %get-tuple-element.7.flow_in), custom_call_target="tpu_custom_call" | custom-call | tf_op jit(solution)/shard_map/deliver/pallas_call | solution.py:468
Async XLA Ops:
  0.6 0.7 %copy-start.2 = (s32[1,1,640]{2,1,0:T(1,128)S(1)}, s32[1,1,640]{2,1,0:T(1,128)}, u32[]{:S(2)}) copy-start(s32[1,1,640]{2,1,0:T(1,128)} %refs_3_.1) | copy-start | bytes 7684
  0.6 0.7 %copy-start.4 = (f32[8]{0:T(128)S(1)}, f32[8]{0:T(128)}, u32[]{:S(2)}) copy-start(f32[8]{0:T(128)} %refs_2_.1) | copy-start | bytes 100
  1.3 1.0 %copy-start = (f32[1,3,8,32,128]{4,3,2,1,0:T(8,128)S(1)}, f32[1,3,8,32,128]{4,3,2,1,0:T(8,128)}, u32[]{:S(2)}) copy-start(f32[1,3,8,32,128]{4,3,2,1,0:T(8,128)} %param.6) | copy-start | bytes 1179652
  2.3 0.9 %copy-start.1 = (f32[1,8,32,128]{3,2,1,0:T(8,128)S(1)}, f32[1,8,32,128]{3,2,1,0:T(8,128)}, u32[]{:S(2)}) copy-start(f32[1,8,32,128]{3,2,1,0:T(8,128)} %param.5) | copy-start | bytes 393220
  3.2 0.7 %copy-start.3 = (f32[1,1,320]{2,1,0:T(1,128)S(1)}, f32[1,1,320]{2,1,0:T(1,128)}, u32[]{:S(2)}) copy-start(f32[1,1,320]{2,1,0:T(1,128)} %refs_4_.1) | copy-start | bytes 3844

commit v4 on v3

--- a/solution.py
+++ b/solution.py
@@ -394,24 +394,14 @@
         result.wait()
 
 
-def deliver(heat_in, flow_in, heat_out, flow_out, heat, flow, sem):
-    size = LEVELS * ROWS
-    pieces = [(heat_in, heat, heat_out, pl.ds(0, size))]
-    pieces += [(flow_in, flow, flow_out, pl.ds(i * size, size)) for i in range(3)]
-    into = [
-        pltpu.make_async_copy(src.at[span], held.at[span], sem.at[0, n])
-        for n, (src, held, _, span) in enumerate(pieces)
+def deliver(heat_in, flow_in, heat_out, flow_out, sem):
+    copies = [
+        pltpu.make_async_copy(heat_in, heat_out, sem.at[0]),
+        pltpu.make_async_copy(flow_in, flow_out, sem.at[1]),
     ]
-    out = [
-        pltpu.make_async_copy(held.at[span], dst.at[span], sem.at[1, n])
-        for n, (_, held, dst, span) in enumerate(pieces)
-    ]
-    for copy in into:
+    for copy in copies:
         copy.start()
-    for first, second in zip(into, out):
-        first.wait()
-        second.start()
-    for copy in out:
+    for copy in copies:
         copy.wait()
 
 
@@ -425,7 +415,7 @@
     step = pl.pallas_call(
         lambda *refs: kernel(n_colat, n_lon, *refs),
         out_shape=(heat_shape, flow_shape),
-        in_specs=[anywhere] * 5,
+        in_specs=[pl.BlockSpec(memory_space=pltpu.HBM)] * 5,
         out_specs=(anywhere, anywhere),
         scratch_shapes=[
             pltpu.VMEM(heat_shape.shape, jnp.float32),
@@ -454,12 +444,8 @@
         deliver,
         out_shape=(heat_shape, flow_shape),
         in_specs=[anywhere] * 2,
-        out_specs=(anywhere, anywhere),
-        scratch_shapes=[
-            pltpu.VMEM(heat_shape.shape, jnp.float32),
-            pltpu.VMEM(flow_shape.shape, jnp.float32),
-            pltpu.SemaphoreType.DMA((2, 4)),
-        ],
+        out_specs=(pl.BlockSpec(memory_space=pltpu.HBM),) * 2,
+        scratch_shapes=[pltpu.SemaphoreType.DMA((2,))],
         compiler_params=pltpu.CompilerParams(vmem_limit_bytes=4 << 20),
         name="deliver",
     )

time: 45.3 us -> 44.5 us (0.982)
  Pallas kernels: 41.2 us -> 40.4 us
    pallas_call x1, Pallas kernels: 1.53 us -> 0.81 us  [on_device(): place(*step(heat.reshape(heat_shape.shape), flow.reshape(flow_shape.shape...]
where the time goes in v4:
time: 44.5 us; the launch traced here: 44.3 us
  Pallas kernels  40.4 us (91%)
  local copies, waits for them, and re-layouts  3.25 us (7%)
  between operations  0.66 us (1%)
    pallas_call x1, Pallas kernels, on_device(): step(heat.reshape(heat_shape.shape), flow.reshape(flow_shape.shape), stif...  39.6 us
    unnamed x10, local copies, waits for them, and re-layouts  3.25 us

profile of v4, /device:TPU:6, one launch (start us, length us, event | category | flops | bytes accessed | tf_op | source)
XLA Modules:
  0.0 44.3 jit_solution(11940622990216748341)
XLA Ops:
  0.6 0.0 copy-start.2
  0.6 0.0 copy-start.4
  0.7 0.7 %copy-done.2 = s32[1,1,640]{2,1,0:T(1,128)S(1)} copy-done((s32[1,1,640]{2,1,0:T(1,128)S(1)}, s32[1,1,640]{2,1,0:T(1,128)}, u32[]{:S(2)}) %copy-start.2) | copy-done | bytes 2584
  1.3 0.0 copy-done.4
  1.3 0.0 copy-start
  1.3 1.0 %copy-done = f32[1,3,8,32,128]{4,3,2,1,0:T(8,128)S(1)} copy-done((f32[1,3,8,32,128]{4,3,2,1,0:T(8,128)S(1)}, f32[1,3,8,32,128]{4,3,2,1,0:T(8,128)}, u32[]{:S(2)}) %copy-start) | copy-done | bytes 393240
  2.3 0.0 copy-start.1
  2.3 0.9 %copy-done.1 = f32[1,8,32,128]{3,2,1,0:T(8,128)S(1)} copy-done((f32[1,8,32,128]{3,2,1,0:T(8,128)S(1)}, f32[1,8,32,128]{3,2,1,0:T(8,128)}, u32[]{:S(2)}) %copy-start.1) | copy-done | bytes 131096
  3.2 0.0 copy-start.3
  3.2 0.7 %copy-done.3 = f32[1,1,320]{2,1,0:T(1,128)S(1)} copy-done((f32[1,1,320]{2,1,0:T(1,128)S(1)}, f32[1,1,320]{2,1,0:T(1,128)}, u32[]{:S(2)}) %copy-start.3) | copy-done | bytes 1304
  3.9 39.6 %mantle_step.1 = (f32[256,128]{1,0:T(8,128)S(1)}, f32[768,128]{1,0:T(8,128)S(1)}) custom-call(f32[256,128]{1,0:T(8,128)S(1)} %bitcast.5, f32[768,128]{1,0:T(8,128)S(1)} %bitcast.4, f32[8]{0:T(128)S(1)} %copy-done.4, s32[1,1,640]{2,1,0:T(1,128)S(1)} %copy-done.2, f32[1,1,320]{2,1,0:T(1,128)S(1)} %copy-done.3), custom_call_target="tpu_custom_call" | custom-call | tf_op jit(solution)/shard_map/mantle_step/pallas_call | solution.py:455
  43.5 0.8 %deliver.1 = (f32[256,128]{1,0:T(8,128)}, f32[768,128]{1,0:T(8,128)}) custom-call(f32[256,128]{1,0:T(8,128)S(1)} %get-tuple-element.6.heat_in, f32[768,128]{1,0:T(8,128)S(1)} %get-tuple-element.7.flow_in), custom_call_target="tpu_custom_call" | custom-call | tf_op jit(solution)/shard_map/deliver/pallas_call | solution.py:454
Async XLA Ops:
  0.6 0.7 %copy-start.2 = (s32[1,1,640]{2,1,0:T(1,128)S(1)}, s32[1,1,640]{2,1,0:T(1,128)}, u32[]{:S(2)}) copy-start(s32[1,1,640]{2,1,0:T(1,128)} %refs_3_.1) | copy-start | bytes 7684
  0.6 0.7 %copy-start.4 = (f32[8]{0:T(128)S(1)}, f32[8]{0:T(128)}, u32[]{:S(2)}) copy-start(f32[8]{0:T(128)} %refs_2_.1) | copy-start | bytes 100
  1.3 1.0 %copy-start = (f32[1,3,8,32,128]{4,3,2,1,0:T(8,128)S(1)}, f32[1,3,8,32,128]{4,3,2,1,0:T(8,128)}, u32[]{:S(2)}) copy-start(f32[1,3,8,32,128]{4,3,2,1,0:T(8,128)} %param.6) | copy-start | bytes 1179652
  2.3 0.9 %copy-start.1 = (f32[1,8,32,128]{3,2,1,0:T(8,128)S(1)}, f32[1,8,32,128]{3,2,1,0:T(8,128)}, u32[]{:S(2)}) copy-start(f32[1,8,32,128]{3,2,1,0:T(8,128)} %param.5) | copy-start | bytes 393220
  3.2 0.7 %copy-start.3 = (f32[1,1,320]{2,1,0:T(1,128)S(1)}, f32[1,1,320]{2,1,0:T(1,128)}, u32[]{:S(2)}) copy-start(f32[1,1,320]{2,1,0:T(1,128)} %refs_4_.1) | copy-start | bytes 3844

commit v5 on v4

--- a/solution.py
+++ b/solution.py
@@ -289,24 +289,38 @@
 
         return rows
 
-    def send_edges(k, par, even, odd):
+    def send_edges(k, par, even, odd, heat=None):
         above = [coef * halo_ns[k, 0, i] for i in range(3)]
         below = [coef * halo_ns[k, 1, i] for i in range(3)]
         last, first = coef * halo_we[k, 0, 0], coef * halo_we[k, 1, 0]
         for i in range(3):
             even = even + shift(jnp.where(on_edge, above[i], 0.0), i * ROWS)
             odd = odd + shift(jnp.where(on_edge, below[i], 0.0), i * ROWS + ROWS - 1)
-        send_we[k + 1, 0, 0] = jnp.where(is_even, even, odd) + shift(last, 1)
-        send_we[k + 1, 1, 0] = jnp.where(is_even, odd, even) + shift(first, -1)
+        to_west, to_east = shift(last, 1), shift(first, -1)
+        if heat is not None:
+            heat_rows, heat_cols = heat
+            for r, value in heat_rows.items():
+                part = shift(jnp.where(on_edge, value, 0.0), r)
+                even, odd = (even, odd + part) if r & 1 else (even + part, odd)
+            at_first = lane_take(heat_cols, (4 * lane) & (COLS - 1))
+            at_last = lane_take(heat_cols, (4 * lane + 3) & (COLS - 1))
+            to_west = to_west + jnp.where(lane < ROWS, at_first, 0.0)
+            to_east = to_east + jnp.where(((lane + 1) & (COLS - 1)) < ROWS, at_last, 0.0)
+        send_we[k + 1, 0, 0] = jnp.where(is_even, even, odd) + to_west
+        send_we[k + 1, 1, 0] = jnp.where(is_even, odd, even) + to_east
         for own, r, halo in ((0, 0, above), (1, ROWS - 1, below)):
             for i in range(3):
                 t = i * ROWS + r
-                send_ns[k + 1, own, i] = (
+                value = (
                     flow[r, i]
                     + halo[i]
                     + jnp.where(lane == 0, shift(last, 1 - t), 0.0)
                     + jnp.where(lane == COLS - 1, shift(first, COLS - 1 - t), 0.0)
                 )
+                if i == 0 and heat is not None:
+                    cols = jnp.where(near_edge, shift(heat_cols, -4 * r), 0.0)
+                    value = value + (heat_rows[r] + cols)
+                send_ns[k + 1, own, i] = value
         send_inside(k + 1, par, False)
 
         def patch(values, index):
@@ -317,31 +331,26 @@
                 add = add + jnp.where(at_row == ROWS - 1, lane_take(below[i], at_col), 0.0)
                 add = add + jnp.where(at_col == 0, lane_take(last, (slot - 1) & (COLS - 1)), 0.0)
                 add = add + jnp.where(at_col == COLS - 1, lane_take(first, slot), 0.0)
+                if i == 0 and heat is not None:
+                    for r, value in heat_rows.items():
+                        add = add + jnp.where(at_row == r, lane_take(value, at_col), 0.0)
+                    near = (at_col < 2) | (at_col >= COLS - 2)
+                    cols = lane_take(heat_cols, (4 * at_row + at_col) & (COLS - 1))
+                    add = add + jnp.where(near, cols, 0.0)
                 values[i] = values[i] + add
             return values
 
         send_found(k + 1, par, False, patch)
 
-    relax(first_row)
-    wait_all(0, 0, True)
-
-    def wide_row(r):
-        if r < 0:
-            return halo_ns[0, 0, 5 + r]
-        if r >= ROWS:
-            return halo_ns[0, 1, 3 + r - ROWS]
-        return heat_row(r)
-
-    around = jnp.where((lane & 3) < 2, halo_we[0, 1, 1], halo_we[0, 0, 1])
-    window = [wide_row(r) for r in range(-2, 2)]
+    def or_zero(r):
+        return heat_row(r) if 0 <= r < ROWS else zero
+
     for r in range(ROWS):
-        window.append(wide_row(r + 2))
-        up2, up1, here, down1, down2 = window[r : r + 5]
-        rim = shift(around, -4 * r)
-        west1 = shift(jnp.where(lane == COLS - 1, rim, here), 1)
-        west2 = shift(jnp.where(lane >= COLS - 2, rim, here), 2)
-        east1 = shift(jnp.where(lane == 0, rim, here), -1)
-        east2 = shift(jnp.where(lane < 2, rim, here), -2)
+        up2, up1, here, down1, down2 = (or_zero(r + j) for j in range(-2, 3))
+        west1 = jnp.where(lane < 1, 0.0, shift(here, 1))
+        west2 = jnp.where(lane < 2, 0.0, shift(here, 2))
+        east1 = jnp.where(lane >= COLS - 1, 0.0, shift(here, -1))
+        east2 = jnp.where(lane >= COLS - 2, 0.0, shift(here, -2))
         above = jnp.where(level == LEVELS - 1, here, pltpu.roll(here, LEVELS - 1, 0))
         below = jnp.where(level == 0, here, pltpu.roll(here, 1, 0))
         grad_colat = (8.0 * (down1 - up1) - (down2 - up2)) * (1.0 / 12.0)
@@ -352,13 +361,51 @@
         stepped = here + TIME_STEP * (laplace - advect)
         heat_out[pl.ds(r, LEVELS, stride=ROWS), :] = stepped
         source[r] = buoyancy * stepped
-        flow[r, 0] = flow[r, 0] + source[r]
+    relax(first_row, source)
+    even, odd = pack_all(flow_row)
+    lon_flow = [zero, zero]
+    for r in range(ROWS):
+        part = shift(jnp.where(near_edge, first_row(r, 2), 0.0), 4 * r)
+        lon_flow[r & 1] = lon_flow[r & 1] + part
+    lon_flow = (lon_flow[0] + lon_flow[1]) * (1.0 / 12.0)
+    find(flow_row)
+    wait_all(0, 0, True)
+
+    far, nearby = halo_ns[0, 0, 3], halo_ns[0, 0, 4]
+    heat_rows = {
+        0: TIME_STEP * (nearby + first_row(0, 1) * ((8.0 * nearby - far) * (1.0 / 12.0))),
+        1: (-TIME_STEP / 12.0) * (first_row(1, 1) * nearby),
+    }
+    nearby, far = halo_ns[0, 1, 3], halo_ns[0, 1, 4]
+    heat_rows[ROWS - 2] = (TIME_STEP / 12.0) * (first_row(ROWS - 2, 1) * nearby)
+    heat_rows[ROWS - 1] = TIME_STEP * (
+        nearby - first_row(ROWS - 1, 1) * ((8.0 * nearby - far) * (1.0 / 12.0))
+    )
+    west1, west2 = shift(halo_we[0, 0, 1], 1), shift(halo_we[0, 0, 1], 2)
+    east1, east2 = shift(halo_we[0, 1, 1], -1), shift(halo_we[0, 1, 1], -2)
+    column = lane & 3
+    heat_cols = TIME_STEP * jnp.where(
+        column == 0,
+        west1 + lon_flow * (8.0 * west1 - west2),
+        jnp.where(
+            column == 1,
+            -lon_flow * west2,
+            jnp.where(column == 2, lon_flow * east2, east1 - lon_flow * (8.0 * east1 - east2)),
+        ),
+    )
+    scaled_rows = {r: buoyancy * value for r, value in heat_rows.items()}
+    send_edges(0, 1, even, odd, (scaled_rows, buoyancy * heat_cols))
+    for r in range(ROWS):
+        add = jnp.where(near_edge, shift(heat_cols, -4 * r), 0.0)
+        if r in heat_rows:
+            add = add + heat_rows[r]
+        at = pl.ds(r, LEVELS, stride=ROWS)
+        heat_out[at, :] = heat_out[at, :] + add
+        add = buoyancy * add
+        source[r] = source[r] + add
+        flow[r, 0] = flow[r, 0] + add
     heat_copy = pltpu.make_async_copy(heat_out, heat_done, out_sem.at[3])
     heat_copy.start()
-
-    even, odd = pack_all(flow_row)
-    find(flow_row)
-    send_edges(0, 1, even, odd)
 
     def step(k, carry):
         par = k & 1
@@ -450,10 +497,13 @@
         name="deliver",
     )
 
+    def pinned(*args):
+        return step(*(pltpu.with_memory_space_constraint(a, pltpu.HBM) for a in args))
+
     def on_device(heat, flow, stiffness, site, phase):
         heat_out, flow_out = place(
-            *step(
-                heat.reshape(heat_shape.shape), flow.reshape(flow_shape.shape), stiffness, site, phase
+            *pinned(
+                heat.reshape(heat_shape.shape), flow.reshape(flow_shape.shape), stiffness, site, phase,
             )
         )
         return heat_out.reshape(heat.shape), flow_out.reshape(flow.shape)

time: 44.5 us -> 40.4 us (0.908)
  local copies, waits for them, and re-layouts: 3.25 us -> 0 us
  Pallas kernels: 40.4 us -> 39.6 us
    unnamed x10 -> x0, local copies, waits for them, and re-layouts: 3.25 us -> none
    pallas_call x2, Pallas kernels: 40.4 us -> 39.6 us  [the longest x1 38.8 us: pinned(): step(*(pltpu.with_memory_space_constraint(a, pltpu.HBM) for a in args))]
where the time goes in v5:
time: 40.4 us; the launch traced here: 40.3 us
  Pallas kernels  39.6 us (98%)
  between operations  0.64 us (2%)
    pallas_call x1, Pallas kernels, pinned(): step(*(pltpu.with_memory_space_constraint(a, pltpu.HBM) for a in args))  38.8 us
    pallas_call x1, Pallas kernels, on_device(): place(*pinned(heat.reshape(heat_shape.shape), flow.reshape(flow_shape.sha...  0.81 us

profile of v5, /device:TPU:6, one launch (start us, length us, event | category | flops | bytes accessed | tf_op | source)
XLA Modules:
  0.0 40.3 jit_solution(7748455620251707038)
XLA Ops:
  0.6 38.8 %mantle_step.1 = (f32[256,128]{1,0:T(8,128)S(1)}, f32[768,128]{1,0:T(8,128)S(1)}) custom-call(f32[256,128]{1,0:T(8,128)} %bitcast.5, f32[768,128]{1,0:T(8,128)} %bitcast.4, f32[8]{0:T(128)} %refs_2_.1, s32[1,1,640]{2,1,0:T(1,128)} %refs_3_.1, f32[1,1,320]{2,1,0:T(1,128)} %refs_4_.1), custom_call_target="tpu_custom_call" | custom-call | tf_op jit(solution)/shard_map/mantle_step/pallas_call | solution.py:501
  39.5 0.8 %deliver.1 = (f32[256,128]{1,0:T(8,128)}, f32[768,128]{1,0:T(8,128)}) custom-call(f32[256,128]{1,0:T(8,128)S(1)} %get-tuple-element.6.heat_in, f32[768,128]{1,0:T(8,128)S(1)} %get-tuple-element.7.flow_in), custom_call_target="tpu_custom_call" | custom-call | tf_op jit(solution)/shard_map/deliver/pallas_call | solution.py:504

commit v6 on v5

--- a/solution.py
+++ b/solution.py
@@ -20,9 +20,9 @@
 def kernel(
     n_colat, n_lon,
     heat_hbm, flow_hbm, stiff_hbm, site_hbm, phase_hbm,
-    heat_done, flow_done,
-    heat_in, flow_in, stiff_in, site_in, phase_in, heat_out, flow_out, in_sem, out_sem,
-    flow, source, found, send_ns, send_we, halo_ns, halo_we, send_sem, recv_sem,
+    heat_out, flow_out,
+    heat_in, flow_in, stiff_in, site_in, phase_in, in_sem,
+    flow, heat, source, found, send_ns, send_we, halo_ns, halo_we, send_sem, recv_sem,
 ):
     p, c, l = (lax.axis_index(a) for a in ("panel", "colat", "lon"))
     lane = lax.broadcasted_iota(jnp.int32, (LEVELS, COLS), 1)
@@ -55,7 +55,7 @@
             )
         )
     ]
-    for n in (3, 4, 0, 1, 2):
+    for n in (1, 2, 0, 3, 4):
         inputs[n].start()
     for n in (0, 1, 2):
         inputs[n].wait()
@@ -99,7 +99,7 @@
     we_angle = lane_take(tail, pick(west, 0, ROWS) + slot_row)
 
     def heat_row(r):
-        return heat_in[pl.ds(r, LEVELS, stride=ROWS), :]
+        return heat[r]
 
     def collect(index, rows, count):
         at_row, at_col = index >> 7, index & (COLS - 1)
@@ -198,8 +198,8 @@
             def _():
                 start(k, par, first, 3)
 
-    def send_inside(k, par, first):
-        for side in (2, 3, 0, 1):
+    def send_inside(k, par, first, which=(2, 3, 0, 1)):
+        for side in which:
 
             @pl.when(at_rim[side] == 0)
             def _(side=side):
@@ -217,8 +217,13 @@
         found[8], found[9] = jnp.cos(we_angle), jnp.sin(we_angle)
 
     inputs[3].wait()
-    even, odd = pack_all(first_row)
+    for r in range(ROWS):
+        for i in range(3):
+            flow[r, i] = first_row(r, i)
+    even, odd = pack_all(flow_row)
     inputs[4].wait()
+    for r in range(ROWS):
+        heat[r] = heat_in[pl.ds(r, LEVELS, stride=ROWS), :]
     near_edge = (lane < 2) | (lane >= COLS - 2)
     heat_packed = [zero, zero]
     for r in range(ROWS):
@@ -230,8 +235,8 @@
         send_ns[0, 1, 3 + j] = heat_row(ROWS - 2 + j)
         send_we[0, j, 1] = heat_packed
     for i in range(3):
-        send_ns[0, 0, i] = first_row(0, i)
-        send_ns[0, 1, i] = first_row(ROWS - 1, i)
+        send_ns[0, 0, i] = flow[0, i]
+        send_ns[0, 1, i] = flow[ROWS - 1, i]
     send_we[0, 0, 0] = jnp.where(is_even, even, odd)
     send_we[0, 1, 0] = jnp.where(is_even, odd, even)
 
@@ -247,7 +252,7 @@
     def _():
         send_we[0, east, 1] = collect(we_heat, lambda r, _: heat_row(r), 1)[0]
 
-    find(first_row)
+    find(flow_row)
     send_found(0, 0, True, lambda values, index: values)
 
     def relax(rows, source=None):
@@ -308,6 +313,7 @@
             to_east = to_east + jnp.where(((lane + 1) & (COLS - 1)) < ROWS, at_last, 0.0)
         send_we[k + 1, 0, 0] = jnp.where(is_even, even, odd) + to_west
         send_we[k + 1, 1, 0] = jnp.where(is_even, odd, even) + to_east
+        send_inside(k + 1, par, False, (2, 3))
         for own, r, halo in ((0, 0, above), (1, ROWS - 1, below)):
             for i in range(3):
                 t = i * ROWS + r
@@ -321,7 +327,7 @@
                     cols = jnp.where(near_edge, shift(heat_cols, -4 * r), 0.0)
                     value = value + (heat_rows[r] + cols)
                 send_ns[k + 1, own, i] = value
-        send_inside(k + 1, par, False)
+        send_inside(k + 1, par, False, (0, 1))
 
         def patch(values, index):
             at_row, at_col = index >> 7, index & (COLS - 1)
@@ -357,17 +363,17 @@
         grad_lon = (8.0 * (east1 - west1) - (east2 - west2)) * (1.0 / 12.0)
         grad_rad = (above - below) * 0.5
         laplace = down1 + up1 + east1 + west1 + above + below - 6.0 * here
-        advect = first_row(r, 0) * grad_rad + first_row(r, 1) * grad_colat + first_row(r, 2) * grad_lon
+        advect = flow[r, 0] * grad_rad + flow[r, 1] * grad_colat + flow[r, 2] * grad_lon
         stepped = here + TIME_STEP * (laplace - advect)
         heat_out[pl.ds(r, LEVELS, stride=ROWS), :] = stepped
         source[r] = buoyancy * stepped
-    relax(first_row, source)
-    even, odd = pack_all(flow_row)
     lon_flow = [zero, zero]
     for r in range(ROWS):
-        part = shift(jnp.where(near_edge, first_row(r, 2), 0.0), 4 * r)
+        part = shift(jnp.where(near_edge, flow[r, 2], 0.0), 4 * r)
         lon_flow[r & 1] = lon_flow[r & 1] + part
     lon_flow = (lon_flow[0] + lon_flow[1]) * (1.0 / 12.0)
+    relax(flow_row, source)
+    even, odd = pack_all(flow_row)
     find(flow_row)
     wait_all(0, 0, True)
 
@@ -404,20 +410,18 @@
         add = buoyancy * add
         source[r] = source[r] + add
         flow[r, 0] = flow[r, 0] + add
-    heat_copy = pltpu.make_async_copy(heat_out, heat_done, out_sem.at[3])
-    heat_copy.start()
 
     def step(k, carry):
         par = k & 1
         relax(completed(k - 1), source)
         even, odd = pack_all(flow_row)
         find(flow_row)
-        wait_all(k, par, False)
 
         @pl.when(k > 1)
         def _():
             wait_sent(k - 1, 1 - par, False)
 
+        wait_all(k, par, False)
         send_edges(k, 1 - par, even, odd)
         return carry
 
@@ -427,18 +431,11 @@
     last_par = (ITERS - 1) & 1
     wait_all(ITERS - 1, last_par, False)
     rows = completed(ITERS - 1)
-    results = []
-    for i in range(3):
-        for r in range(ROWS):
+    for r in range(ROWS):
+        for i in range(3):
             flow_out[pl.ds(i * LEVELS * ROWS + r, LEVELS, stride=ROWS), :] = rows(r, i)
-        span = pl.ds(i * LEVELS * ROWS, LEVELS * ROWS)
-        results.append(pltpu.make_async_copy(flow_out.at[span], flow_done.at[span], out_sem.at[i]))
-        results[-1].start()
     wait_sent(ITERS - 2, 1 - last_par, False)
     wait_sent(ITERS - 1, last_par, False)
-    heat_copy.wait()
-    for result in results:
-        result.wait()
 
 
 def deliver(heat_in, flow_in, heat_out, flow_out, sem):
@@ -463,18 +460,16 @@
         lambda *refs: kernel(n_colat, n_lon, *refs),
         out_shape=(heat_shape, flow_shape),
         in_specs=[pl.BlockSpec(memory_space=pltpu.HBM)] * 5,
-        out_specs=(anywhere, anywhere),
+        out_specs=(pl.BlockSpec(memory_space=pltpu.VMEM),) * 2,
         scratch_shapes=[
             pltpu.VMEM(heat_shape.shape, jnp.float32),
             pltpu.VMEM(flow_shape.shape, jnp.float32),
             pltpu.SMEM((LEVELS,), jnp.float32),
             pltpu.VMEM((1, 1, 4 * (COLS + ROWS)), jnp.int32),
             pltpu.VMEM((1, 1, 2 * (COLS + ROWS)), jnp.float32),
-            pltpu.VMEM(heat_shape.shape, jnp.float32),
-            pltpu.VMEM(flow_shape.shape, jnp.float32),
             pltpu.SemaphoreType.DMA((5,)),
-            pltpu.SemaphoreType.DMA((4,)),
             pltpu.VMEM((ROWS, 3, *block), jnp.float32),
+            pltpu.VMEM((ROWS, *block), jnp.float32),
             pltpu.VMEM((ROWS, *block), jnp.float32),
             pltpu.VMEM((10, *block), jnp.float32),
             pltpu.VMEM((ITERS, 2, 5, *block), jnp.float32),

time: 40.4 us -> 39.5 us (0.978)
  Pallas kernels: 39.6 us -> 38.7 us
    pallas_call x1, Pallas kernels: 38.8 us -> 37.9 us  [pinned(): step(*(pltpu.with_memory_space_constraint(a, pltpu.HBM) for a in args))]
where the time goes in v6:
time: 39.5 us; the launch traced here: 39.4 us
  Pallas kernels  38.7 us (98%)
  between operations  0.64 us (2%)
    pallas_call x1, Pallas kernels, pinned(): step(*(pltpu.with_memory_space_constraint(a, pltpu.HBM) for a in args))  37.9 us
    pallas_call x1, Pallas kernels, on_device(): place(*pinned(heat.reshape(heat_shape.shape), flow.reshape(flow_shape.sha...  0.81 us

profile of v6, /device:TPU:6, one launch (start us, length us, event | category | flops | bytes accessed | tf_op | source)
XLA Modules:
  0.0 39.4 jit_solution(17242752885208648796)
XLA Ops:
  0.6 37.9 %mantle_step.1 = (f32[256,128]{1,0:T(8,128)S(1)}, f32[768,128]{1,0:T(8,128)S(1)}) custom-call(f32[256,128]{1,0:T(8,128)} %bitcast.5, f32[768,128]{1,0:T(8,128)} %bitcast.4, f32[8]{0:T(128)} %refs_2_.1, s32[1,1,640]{2,1,0:T(1,128)} %refs_3_.1, f32[1,1,320]{2,1,0:T(1,128)} %refs_4_.1), custom_call_target="tpu_custom_call" | custom-call | tf_op jit(solution)/shard_map/mantle_step/pallas_call | solution.py:496
  38.5 0.8 %deliver.1 = (f32[256,128]{1,0:T(8,128)}, f32[768,128]{1,0:T(8,128)}) custom-call(f32[256,128]{1,0:T(8,128)S(1)} %get-tuple-element.6.heat_in, f32[768,128]{1,0:T(8,128)S(1)} %get-tuple-element.7.flow_in), custom_call_target="tpu_custom_call" | custom-call | tf_op jit(solution)/shard_map/deliver/pallas_call | solution.py:499

commit v7 on v6

--- a/solution.py
+++ b/solution.py
@@ -21,7 +21,7 @@
     n_colat, n_lon,
     heat_hbm, flow_hbm, stiff_hbm, site_hbm, phase_hbm,
     heat_out, flow_out,
-    heat_in, flow_in, stiff_in, site_in, phase_in, in_sem,
+    stiff_in, site_in, phase_in, in_sem,
     flow, heat, source, found, send_ns, send_we, halo_ns, halo_we, send_sem, recv_sem,
 ):
     p, c, l = (lax.axis_index(a) for a in ("panel", "colat", "lon"))
@@ -43,22 +43,21 @@
     barrier = pltpu.get_barrier_semaphore()
     for device, _ in sides:
         pl.semaphore_signal(barrier, inc=1, device_id=device, device_id_type=MESH)
-    inputs = [
+    small = [
         pltpu.make_async_copy(src, dst, in_sem.at[n])
         for n, (src, dst) in enumerate(
-            (
-                (stiff_hbm, stiff_in),
-                (site_hbm, site_in),
-                (phase_hbm, phase_in),
-                (flow_hbm, flow_in),
-                (heat_hbm, heat_in),
-            )
+            ((site_hbm, site_in), (phase_hbm, phase_in), (stiff_hbm, stiff_in))
         )
     ]
-    for n in (1, 2, 0, 3, 4):
-        inputs[n].start()
-    for n in (0, 1, 2):
-        inputs[n].wait()
+    for copy in small:
+        copy.start()
+    for i in range(3):
+        for k in range(LEVELS):
+            pltpu.make_async_copy(flow_hbm.at[i, k], flow.at[:, i, k, :], in_sem.at[3]).start()
+    for k in range(LEVELS):
+        pltpu.make_async_copy(heat_hbm.at[k], heat.at[:, k, :], in_sem.at[4]).start()
+    for copy in small:
+        copy.wait()
 
     stiff = jnp.zeros((LEVELS, COLS), jnp.float32)
     for k in range(LEVELS):
@@ -205,9 +204,6 @@
             def _(side=side):
                 start(k, par, first, side)
 
-    def first_row(r, i):
-        return flow_in[pl.ds(i * LEVELS * ROWS + r, LEVELS, stride=ROWS), :]
-
     @on_rim(north, south)
     def _():
         found[6], found[7] = jnp.cos(ns_angle), jnp.sin(ns_angle)
@@ -216,14 +212,9 @@
     def _():
         found[8], found[9] = jnp.cos(we_angle), jnp.sin(we_angle)
 
-    inputs[3].wait()
-    for r in range(ROWS):
-        for i in range(3):
-            flow[r, i] = first_row(r, i)
+    pltpu.make_async_copy(flow, flow, in_sem.at[3]).wait()
     even, odd = pack_all(flow_row)
-    inputs[4].wait()
-    for r in range(ROWS):
-        heat[r] = heat_in[pl.ds(r, LEVELS, stride=ROWS), :]
+    pltpu.make_async_copy(heat, heat, in_sem.at[4]).wait()
     near_edge = (lane < 2) | (lane >= COLS - 2)
     heat_packed = [zero, zero]
     for r in range(ROWS):
@@ -365,8 +356,9 @@
         laplace = down1 + up1 + east1 + west1 + above + below - 6.0 * here
         advect = flow[r, 0] * grad_rad + flow[r, 1] * grad_colat + flow[r, 2] * grad_lon
         stepped = here + TIME_STEP * (laplace - advect)
-        heat_out[pl.ds(r, LEVELS, stride=ROWS), :] = stepped
+        heat_out[r] = stepped
         source[r] = buoyancy * stepped
+    outer_flow = {r: flow[r, 1] for r in (0, 1, ROWS - 2, ROWS - 1)}
     lon_flow = [zero, zero]
     for r in range(ROWS):
         part = shift(jnp.where(near_edge, flow[r, 2], 0.0), 4 * r)
@@ -379,13 +371,13 @@
 
     far, nearby = halo_ns[0, 0, 3], halo_ns[0, 0, 4]
     heat_rows = {
-        0: TIME_STEP * (nearby + first_row(0, 1) * ((8.0 * nearby - far) * (1.0 / 12.0))),
-        1: (-TIME_STEP / 12.0) * (first_row(1, 1) * nearby),
+        0: TIME_STEP * (nearby + outer_flow[0] * ((8.0 * nearby - far) * (1.0 / 12.0))),
+        1: (-TIME_STEP / 12.0) * (outer_flow[1] * nearby),
     }
     nearby, far = halo_ns[0, 1, 3], halo_ns[0, 1, 4]
-    heat_rows[ROWS - 2] = (TIME_STEP / 12.0) * (first_row(ROWS - 2, 1) * nearby)
+    heat_rows[ROWS - 2] = (TIME_STEP / 12.0) * (outer_flow[ROWS - 2] * nearby)
     heat_rows[ROWS - 1] = TIME_STEP * (
-        nearby - first_row(ROWS - 1, 1) * ((8.0 * nearby - far) * (1.0 / 12.0))
+        nearby - outer_flow[ROWS - 1] * ((8.0 * nearby - far) * (1.0 / 12.0))
     )
     west1, west2 = shift(halo_we[0, 0, 1], 1), shift(halo_we[0, 0, 1], 2)
     east1, east2 = shift(halo_we[0, 1, 1], -1), shift(halo_we[0, 1, 1], -2)
@@ -405,8 +397,7 @@
         add = jnp.where(near_edge, shift(heat_cols, -4 * r), 0.0)
         if r in heat_rows:
             add = add + heat_rows[r]
-        at = pl.ds(r, LEVELS, stride=ROWS)
-        heat_out[at, :] = heat_out[at, :] + add
+        heat_out[r] = heat_out[r] + add
         add = buoyancy * add
         source[r] = source[r] + add
         flow[r, 0] = flow[r, 0] + add
@@ -433,37 +424,36 @@
     rows = completed(ITERS - 1)
     for r in range(ROWS):
         for i in range(3):
-            flow_out[pl.ds(i * LEVELS * ROWS + r, LEVELS, stride=ROWS), :] = rows(r, i)
+            flow_out[r, i] = rows(r, i)
     wait_sent(ITERS - 2, 1 - last_par, False)
     wait_sent(ITERS - 1, last_par, False)
 
 
 def deliver(heat_in, flow_in, heat_out, flow_out, sem):
-    copies = [
-        pltpu.make_async_copy(heat_in, heat_out, sem.at[0]),
-        pltpu.make_async_copy(flow_in, flow_out, sem.at[1]),
-    ]
-    for copy in copies:
-        copy.start()
-    for copy in copies:
-        copy.wait()
+    for i in range(3):
+        for k in range(LEVELS):
+            pltpu.make_async_copy(flow_in.at[:, i, k, :], flow_out.at[i, k], sem.at[0]).start()
+    for k in range(LEVELS):
+        pltpu.make_async_copy(heat_in.at[:, k, :], heat_out.at[k], sem.at[1]).start()
+    pltpu.make_async_copy(flow_out, flow_out, sem.at[0]).wait()
+    pltpu.make_async_copy(heat_out, heat_out, sem.at[1]).wait()
 
 
 def solution(mesh):
     n_colat, n_lon = mesh.shape["colat"], mesh.shape["lon"]
 
     block = (LEVELS, COLS)
-    heat_shape = jax.ShapeDtypeStruct((LEVELS * ROWS, COLS), jnp.float32)
-    flow_shape = jax.ShapeDtypeStruct((3 * LEVELS * ROWS, COLS), jnp.float32)
+    heat_shape = jax.ShapeDtypeStruct((LEVELS, ROWS, COLS), jnp.float32)
+    flow_shape = jax.ShapeDtypeStruct((3, LEVELS, ROWS, COLS), jnp.float32)
+    heat_by_row = jax.ShapeDtypeStruct((ROWS, *block), jnp.float32)
+    flow_by_row = jax.ShapeDtypeStruct((ROWS, 3, *block), jnp.float32)
     anywhere = pl.BlockSpec(memory_space=pl.ANY)
     step = pl.pallas_call(
         lambda *refs: kernel(n_colat, n_lon, *refs),
-        out_shape=(heat_shape, flow_shape),
+        out_shape=(heat_by_row, flow_by_row),
         in_specs=[pl.BlockSpec(memory_space=pltpu.HBM)] * 5,
         out_specs=(pl.BlockSpec(memory_space=pltpu.VMEM),) * 2,
         scratch_shapes=[
-            pltpu.VMEM(heat_shape.shape, jnp.float32),
-            pltpu.VMEM(flow_shape.shape, jnp.float32),
             pltpu.SMEM((LEVELS,), jnp.float32),
             pltpu.VMEM((1, 1, 4 * (COLS + ROWS)), jnp.int32),
             pltpu.VMEM((1, 1, 2 * (COLS + ROWS)), jnp.float32),

time: 39.5 us -> 39 us (0.987)
  Pallas kernels: 38.7 us -> 38.2 us
    pallas_call x1, Pallas kernels: 37.9 us -> 37.4 us  [pinned(): step(*(pltpu.with_memory_space_constraint(a, pltpu.HBM) for a in args))]
where the time goes in v7:
time: 39 us; the launch traced here: 38.8 us
  Pallas kernels  38.2 us (98%)
  between operations  0.64 us (2%)
    pallas_call x1, Pallas kernels, pinned(): step(*(pltpu.with_memory_space_constraint(a, pltpu.HBM) for a in args))  37.4 us
    pallas_call x1, Pallas kernels, on_device(): place(*pinned(heat.reshape(heat_shape.shape), flow.reshape(flow_shape.sha...  0.79 us

profile of v7, /device:TPU:6, one launch (start us, length us, event | category | flops | bytes accessed | tf_op | source)
XLA Modules:
  0.0 38.8 jit_solution(14377264416495627737)
XLA Ops:
  0.6 37.4 %mantle_step.1 = (f32[32,8,128]{2,1,0:T(8,128)S(1)}, f32[32,3,8,128]{3,2,1,0:T(8,128)S(1)}) custom-call(f32[8,32,128]{2,1,0:T(8,128)} %bitcast.5, f32[3,8,32,128]{3,2,1,0:T(8,128)} %bitcast.4, f32[8]{0:T(128)} %refs_2_.1, s32[1,1,640]{2,1,0:T(1,128)} %refs_3_.1, f32[1,1,320]{2,1,0:T(1,128)} %refs_4_.1), custom_call_target="tpu_custom_call" | custom-call | tf_op jit(solution)/shard_map/mantle_step/pallas_call | solution.py:486
  38.0 0.8 %deliver.1 = (f32[8,32,128]{2,1,0:T(8,128)}, f32[3,8,32,128]{3,2,1,0:T(8,128)}) custom-call(f32[32,8,128]{2,1,0:T(8,128)S(1)} %get-tuple-element.6.heat_in, f32[32,3,8,128]{3,2,1,0:T(8,128)S(1)} %get-tuple-element.7.flow_in), custom_call_target="tpu_custom_call" | custom-call | tf_op jit(solution)/shard_map/deliver/pallas_call | solution.py:489

commit v8 on v7

--- a/solution.py
+++ b/solution.py
@@ -17,10 +17,23 @@
     return jnp.take_along_axis(value, index, axis=1, mode="promise_in_bounds")
 
 
+def with_halo(rows, share, on_edge):
+    def complete(r, i):
+        by = (COLS - 1 - i * ROWS - r) % COLS
+        value = rows(r, i) + jnp.where(on_edge, pltpu.roll(share[6 + (r & 1)], by, 1), 0.0)
+        if r == 0:
+            value = value + share[i]
+        if r == ROWS - 1:
+            value = value + share[3 + i]
+        return value
+
+    return complete
+
+
 def kernel(
     n_colat, n_lon,
     heat_hbm, flow_hbm, stiff_hbm, site_hbm, phase_hbm,
-    heat_out, flow_out,
+    heat_out, flow_out, halo_out,
     stiff_in, site_in, phase_in, in_sem,
     flow, heat, source, found, send_ns, send_we, halo_ns, halo_we, send_sem, recv_sem,
 ):
@@ -246,7 +259,7 @@
     find(flow_row)
     send_found(0, 0, True, lambda values, index: values)
 
-    def relax(rows, source=None):
+    def relax(rows, source=None, result=flow):
         before = [zero] * 3
         now = [rows(0, i) for i in range(3)]
         for r in range(ROWS):
@@ -265,25 +278,18 @@
                 )
                 if i == 0 and source is not None:
                     value = value + source[r]
-                flow[r, i] = value
+                result[r, i] = value
             before, now = now, after
 
+    def halo_share(k):
+        first_cols, last_cols = halo_we[k, 1, 0], shift(halo_we[k, 0, 0], 2)
+        share = [coef * halo_ns[k, side, i] for side in range(2) for i in range(3)]
+        share.append(coef * jnp.where(is_even, first_cols, last_cols))
+        share.append(coef * jnp.where(is_even, last_cols, first_cols))
+        return share
+
     def completed(k):
-        first_cols, last_cols = halo_we[k, 1, 0], shift(halo_we[k, 0, 0], 2)
-        pair = (
-            coef * jnp.where(is_even, first_cols, last_cols),
-            coef * jnp.where(is_even, last_cols, first_cols),
-        )
-
-        def rows(r, i):
-            value = flow[r, i] + jnp.where(on_edge, shift(pair[r & 1], COLS - 1 - i * ROWS - r), 0.0)
-            if r == 0:
-                value = value + coef * halo_ns[k, 0, i]
-            if r == ROWS - 1:
-                value = value + coef * halo_ns[k, 1, i]
-            return value
-
-        return rows
+        return with_halo(lambda r, i: flow[r, i], halo_share(k), on_edge)
 
     def send_edges(k, par, even, odd, heat=None):
         above = [coef * halo_ns[k, 0, i] for i in range(3)]
@@ -418,25 +424,35 @@
 
     wait_sent(0, 0, True)
     lax.fori_loop(1, ITERS - 1, step, 0)
-    relax(completed(ITERS - 2), source)
+    relax(completed(ITERS - 2), source, flow_out)
     last_par = (ITERS - 1) & 1
+    wait_sent(ITERS - 2, 1 - last_par, False)
+    wait_sent(ITERS - 1, last_par, False)
     wait_all(ITERS - 1, last_par, False)
-    rows = completed(ITERS - 1)
+    for n, value in enumerate(halo_share(ITERS - 1)):
+        halo_out[n] = value
+
+
+def deliver(heat_in, flow_in, halo_in, heat_out, flow_out, done, sem):
+    for k in range(LEVELS):
+        pltpu.make_async_copy(heat_in.at[:, k, :], heat_out.at[k], sem.at[0]).start()
+    lane = lax.broadcasted_iota(jnp.int32, (LEVELS, COLS), 1)
+    on_edge = (lane == 0) | (lane == COLS - 1)
+    rows = with_halo(lambda r, i: flow_in[r, i], [halo_in[n] for n in range(8)], on_edge)
+
+    def send(r):
+        pltpu.make_async_copy(done.at[r], flow_out.at[:, :, r, :], sem.at[1]).start()
+
+    lag = 4
     for r in range(ROWS):
         for i in range(3):
-            flow_out[r, i] = rows(r, i)
-    wait_sent(ITERS - 2, 1 - last_par, False)
-    wait_sent(ITERS - 1, last_par, False)
-
-
-def deliver(heat_in, flow_in, heat_out, flow_out, sem):
-    for i in range(3):
-        for k in range(LEVELS):
-            pltpu.make_async_copy(flow_in.at[:, i, k, :], flow_out.at[i, k], sem.at[0]).start()
-    for k in range(LEVELS):
-        pltpu.make_async_copy(heat_in.at[:, k, :], heat_out.at[k], sem.at[1]).start()
-    pltpu.make_async_copy(flow_out, flow_out, sem.at[0]).wait()
-    pltpu.make_async_copy(heat_out, heat_out, sem.at[1]).wait()
+            done[r, i] = rows(r, i)
+        if r >= lag:
+            send(r - lag)
+    for r in range(ROWS - lag, ROWS):
+        send(r)
+    pltpu.make_async_copy(heat_out, heat_out, sem.at[0]).wait()
+    pltpu.make_async_copy(flow_out, flow_out, sem.at[1]).wait()
 
 
 def solution(mesh):
@@ -446,13 +462,14 @@
     heat_shape = jax.ShapeDtypeStruct((LEVELS, ROWS, COLS), jnp.float32)
     flow_shape = jax.ShapeDtypeStruct((3, LEVELS, ROWS, COLS), jnp.float32)
     heat_by_row = jax.ShapeDtypeStruct((ROWS, *block), jnp.float32)
+    halo_shape = jax.ShapeDtypeStruct((8, *block), jnp.float32)
+    vmem = pl.BlockSpec(memory_space=pltpu.VMEM)
     flow_by_row = jax.ShapeDtypeStruct((ROWS, 3, *block), jnp.float32)
-    anywhere = pl.BlockSpec(memory_space=pl.ANY)
     step = pl.pallas_call(
         lambda *refs: kernel(n_colat, n_lon, *refs),
-        out_shape=(heat_by_row, flow_by_row),
+        out_shape=(heat_by_row, flow_by_row, halo_shape),
         in_specs=[pl.BlockSpec(memory_space=pltpu.HBM)] * 5,
-        out_specs=(pl.BlockSpec(memory_space=pltpu.VMEM),) * 2,
+        out_specs=(vmem,) * 3,
         scratch_shapes=[
             pltpu.SMEM((LEVELS,), jnp.float32),
             pltpu.VMEM((1, 1, 4 * (COLS + ROWS)), jnp.int32),
@@ -475,9 +492,12 @@
     place = pl.pallas_call(
         deliver,
         out_shape=(heat_shape, flow_shape),
-        in_specs=[anywhere] * 2,
+        in_specs=[vmem] * 3,
         out_specs=(pl.BlockSpec(memory_space=pltpu.HBM),) * 2,
-        scratch_shapes=[pltpu.SemaphoreType.DMA((2,))],
+        scratch_shapes=[
+            pltpu.VMEM(flow_by_row.shape, jnp.float32),
+            pltpu.SemaphoreType.DMA((2,)),
+        ],
         compiler_params=pltpu.CompilerParams(vmem_limit_bytes=4 << 20),
         name="deliver",
     )

time: 39 us -> 38.8 us (level)
  no operation moved by 1% of the time
where the time goes in v8:
time: 38.8 us; the launch traced here: 38.7 us
  Pallas kernels  38 us (98%)
  between operations  0.64 us (2%)
    pallas_call x1, Pallas kernels, pinned(): step(*(pltpu.with_memory_space_constraint(a, pltpu.HBM) for a in args))  37.2 us
    pallas_call x1, Pallas kernels, on_device(): place(*pinned(heat.reshape(heat_shape.shape), flow.reshape(flow_shape.sha...  0.82 us

profile of v8, /device:TPU:6, one launch (start us, length us, event | category | flops | bytes accessed | tf_op | source)
XLA Modules:
  0.0 38.7 jit_solution(16516312159782307480)
XLA Ops:
  0.6 37.2 %mantle_step.1 = (f32[32,8,128]{2,1,0:T(8,128)S(1)}, f32[32,3,8,128]{3,2,1,0:T(8,128)S(1)}, f32[8,8,128]{2,1,0:T(8,128)S(1)}) custom-call(f32[8,32,128]{2,1,0:T(8,128)} %bitcast.5, f32[3,8,32,128]{3,2,1,0:T(8,128)} %bitcast.4, f32[8]{0:T(128)} %refs_2_.1, s32[1,1,640]{2,1,0:T(1,128)} %refs_3_.1, f32[1,1,320]{2,1,0:T(1,128)} %refs_4_.1), custom_call_target="tpu_custom_call" | custom-call | tf_op jit(solution)/shard_map/mantle_step/pallas_call | solution.py:506
  37.9 0.8 %deliver.1 = (f32[8,32,128]{2,1,0:T(8,128)}, f32[3,8,32,128]{3,2,1,0:T(8,128)}) custom-call(f32[32,8,128]{2,1,0:T(8,128)S(1)} %get-tuple-element.7.heat_in, f32[32,3,8,128]{3,2,1,0:T(8,128)S(1)} %get-tuple-element.8.flow_in, f32[8,8,128]{2,1,0:T(8,128)S(1)} %get-tuple-element.9.halo_in), custom_call_target="tpu_custom_call" | custom-call | tf_op jit(solution)/shard_map/deliver/pallas_call | solution.py:509

commit v9 on v8

--- a/solution.py
+++ b/solution.py
@@ -91,8 +91,7 @@
     def pick(flag, yes, no):
         return jnp.where(flag == 1, yes, no)
 
-    slot = (lane + west) & (COLS - 1)
-    slot_row, slot_part = slot & (ROWS - 1), slot >> 5
+    slot_row, slot_part = lane & (ROWS - 1), lane >> 5
     heat_slot = (lane + 2 * west) & (COLS - 1)
 
     def sites(j):
@@ -149,8 +148,8 @@
     def start(k, par, first, side):
         copy(k, par, first, side).start()
 
-    def wait_all(k, par, first):
-        for side in range(4):
+    def wait_all(k, par, first, which=(0, 1, 2, 3)):
+        for side in which:
             copy(k, par, first, side, arriving=True).wait_recv()
 
     def wait_sent(k, par, first):
@@ -242,10 +241,8 @@
         send_ns[0, 0, i] = flow[0, i]
         send_ns[0, 1, i] = flow[ROWS - 1, i]
     send_we[0, 0, 0] = jnp.where(is_even, even, odd)
-    send_we[0, 1, 0] = jnp.where(is_even, odd, even)
-
-    pl.semaphore_wait(barrier, 4)
-    send_inside(0, 0, True)
+    send_we[0, 1, 0] = shift(jnp.where(is_even, odd, even), 1)
+
 
     @on_rim(north, south)
     def _():
@@ -257,6 +254,8 @@
         send_we[0, east, 1] = collect(we_heat, lambda r, _: heat_row(r), 1)[0]
 
     find(flow_row)
+    pl.semaphore_wait(barrier, 4)
+    send_inside(0, 0, True)
     send_found(0, 0, True, lambda values, index: values)
 
     def relax(rows, source=None, result=flow):
@@ -282,7 +281,7 @@
             before, now = now, after
 
     def halo_share(k):
-        first_cols, last_cols = halo_we[k, 1, 0], shift(halo_we[k, 0, 0], 2)
+        first_cols, last_cols = halo_we[k, 1, 0], shift(halo_we[k, 0, 0], 1)
         share = [coef * halo_ns[k, side, i] for side in range(2) for i in range(3)]
         share.append(coef * jnp.where(is_even, first_cols, last_cols))
         share.append(coef * jnp.where(is_even, last_cols, first_cols))
@@ -294,30 +293,34 @@
     def send_edges(k, par, even, odd, heat=None):
         above = [coef * halo_ns[k, 0, i] for i in range(3)]
         below = [coef * halo_ns[k, 1, i] for i in range(3)]
-        last, first = coef * halo_we[k, 0, 0], coef * halo_we[k, 1, 0]
         for i in range(3):
             even = even + shift(jnp.where(on_edge, above[i], 0.0), i * ROWS)
             odd = odd + shift(jnp.where(on_edge, below[i], 0.0), i * ROWS + ROWS - 1)
-        to_west, to_east = shift(last, 1), shift(first, -1)
         if heat is not None:
             heat_rows, heat_cols = heat
             for r, value in heat_rows.items():
                 part = shift(jnp.where(on_edge, value, 0.0), r)
                 even, odd = (even, odd + part) if r & 1 else (even + part, odd)
+        west_edge, east_edge = jnp.where(is_even, even, odd), shift(jnp.where(is_even, odd, even), 1)
+        outer = [[flow[0, i] + above[i] for i in range(3)], [flow[ROWS - 1, i] + below[i] for i in range(3)]]
+        if heat is None:
+            wait_all(k, 1 - par, False, (2, 3))
+        last, first = coef * halo_we[k, 0, 0], coef * halo_we[k, 1, 0]
+        to_west, to_east = last, first
+        if heat is not None:
             at_first = lane_take(heat_cols, (4 * lane) & (COLS - 1))
-            at_last = lane_take(heat_cols, (4 * lane + 3) & (COLS - 1))
+            at_last = lane_take(heat_cols, (4 * lane - 1) & (COLS - 1))
             to_west = to_west + jnp.where(lane < ROWS, at_first, 0.0)
-            to_east = to_east + jnp.where(((lane + 1) & (COLS - 1)) < ROWS, at_last, 0.0)
-        send_we[k + 1, 0, 0] = jnp.where(is_even, even, odd) + to_west
-        send_we[k + 1, 1, 0] = jnp.where(is_even, odd, even) + to_east
+            to_east = to_east + jnp.where(lane < ROWS, at_last, 0.0)
+        send_we[k + 1, 0, 0] = west_edge + to_west
+        send_we[k + 1, 1, 0] = east_edge + to_east
         send_inside(k + 1, par, False, (2, 3))
-        for own, r, halo in ((0, 0, above), (1, ROWS - 1, below)):
+        for own, r in ((0, 0), (1, ROWS - 1)):
             for i in range(3):
                 t = i * ROWS + r
                 value = (
-                    flow[r, i]
-                    + halo[i]
-                    + jnp.where(lane == 0, shift(last, 1 - t), 0.0)
+                    outer[own][i]
+                    + jnp.where(lane == 0, shift(last, -t), 0.0)
                     + jnp.where(lane == COLS - 1, shift(first, COLS - 1 - t), 0.0)
                 )
                 if i == 0 and heat is not None:
@@ -332,7 +335,7 @@
                 slot = i * ROWS + at_row
                 add = jnp.where(at_row == 0, lane_take(above[i], at_col), 0.0)
                 add = add + jnp.where(at_row == ROWS - 1, lane_take(below[i], at_col), 0.0)
-                add = add + jnp.where(at_col == 0, lane_take(last, (slot - 1) & (COLS - 1)), 0.0)
+                add = add + jnp.where(at_col == 0, lane_take(last, slot), 0.0)
                 add = add + jnp.where(at_col == COLS - 1, lane_take(first, slot), 0.0)
                 if i == 0 and heat is not None:
                     for r, value in heat_rows.items():
@@ -418,7 +421,7 @@
         def _():
             wait_sent(k - 1, 1 - par, False)
 
-        wait_all(k, par, False)
+        wait_all(k, par, False, (0, 1))
         send_edges(k, 1 - par, even, odd)
         return carry
 

time: 38.8 us -> 39.1 us (level)
  no operation moved by 1% of the time
where the time goes in v9:
time: 39.1 us; the launch traced here: 38.9 us
  Pallas kernels  38.3 us (98%)
  between operations  0.64 us (2%)
    pallas_call x1, Pallas kernels, pinned(): step(*(pltpu.with_memory_space_constraint(a, pltpu.HBM) for a in args))  37.5 us
    pallas_call x1, Pallas kernels, on_device(): place(*pinned(heat.reshape(heat_shape.shape), flow.reshape(flow_shape.sha...  0.82 us

profile of v9, /device:TPU:6, one launch (start us, length us, event | category | flops | bytes accessed | tf_op | source)
XLA Modules:
  0.0 38.9 jit_solution(15859280702682170143)
XLA Ops:
  0.6 37.5 %mantle_step.1 = (f32[32,8,128]{2,1,0:T(8,128)S(1)}, f32[32,3,8,128]{3,2,1,0:T(8,128)S(1)}, f32[8,8,128]{2,1,0:T(8,128)S(1)}) custom-call(f32[8,32,128]{2,1,0:T(8,128)} %bitcast.5, f32[3,8,32,128]{3,2,1,0:T(8,128)} %bitcast.4, f32[8]{0:T(128)} %refs_2_.1, s32[1,1,640]{2,1,0:T(1,128)} %refs_3_.1, f32[1,1,320]{2,1,0:T(1,128)} %refs_4_.1), custom_call_target="tpu_custom_call" | custom-call | tf_op jit(solution)/shard_map/mantle_step/pallas_call | solution.py:509
  38.1 0.8 %deliver.1 = (f32[8,32,128]{2,1,0:T(8,128)}, f32[3,8,32,128]{3,2,1,0:T(8,128)}) custom-call(f32[32,8,128]{2,1,0:T(8,128)S(1)} %get-tuple-element.7.heat_in, f32[32,3,8,128]{3,2,1,0:T(8,128)S(1)} %get-tuple-element.8.flow_in, f32[8,8,128]{2,1,0:T(8,128)S(1)} %get-tuple-element.9.halo_in), custom_call_target="tpu_custom_call" | custom-call | tf_op jit(solution)/shard_map/deliver/pallas_call | solution.py:512

commit v10 on v9

--- a/solution.py
+++ b/solution.py
@@ -180,7 +180,7 @@
         cos, sin = found[angle], found[angle + 1]
         return a, cos * b + sin * d, cos * d - sin * b
 
-    def send_found(k, par, first, patch):
+    def send_found_rows(k, par, first, patch):
         @on_rim(north, south)
         def _():
             values = patch([found[i] for i in range(3)], ns_site)
@@ -195,6 +195,7 @@
             def _():
                 start(k, par, first, 1)
 
+    def send_found_cols(k, par, first, patch):
         @on_rim(west, east)
         def _():
             values = patch([found[3 + i] for i in range(3)], we_site)
@@ -256,7 +257,8 @@
     find(flow_row)
     pl.semaphore_wait(barrier, 4)
     send_inside(0, 0, True)
-    send_found(0, 0, True, lambda values, index: values)
+    send_found_rows(0, 0, True, lambda values, index: values)
+    send_found_cols(0, 0, True, lambda values, index: values)
 
     def relax(rows, source=None, result=flow):
         before = [zero] * 3
@@ -315,19 +317,6 @@
         send_we[k + 1, 0, 0] = west_edge + to_west
         send_we[k + 1, 1, 0] = east_edge + to_east
         send_inside(k + 1, par, False, (2, 3))
-        for own, r in ((0, 0), (1, ROWS - 1)):
-            for i in range(3):
-                t = i * ROWS + r
-                value = (
-                    outer[own][i]
-                    + jnp.where(lane == 0, shift(last, -t), 0.0)
-                    + jnp.where(lane == COLS - 1, shift(first, COLS - 1 - t), 0.0)
-                )
-                if i == 0 and heat is not None:
-                    cols = jnp.where(near_edge, shift(heat_cols, -4 * r), 0.0)
-                    value = value + (heat_rows[r] + cols)
-                send_ns[k + 1, own, i] = value
-        send_inside(k + 1, par, False, (0, 1))
 
         def patch(values, index):
             at_row, at_col = index >> 7, index & (COLS - 1)
@@ -346,7 +335,29 @@
                 values[i] = values[i] + add
             return values
 
-        send_found(k + 1, par, False, patch)
+        send_found_rows(k + 1, par, False, patch)
+        values = ([], [])
+        for own, r in ((0, 0), (1, ROWS - 1)):
+            for i in range(3):
+                t = i * ROWS + r
+                value = (
+                    outer[own][i]
+                    + jnp.where(lane == 0, shift(last, -t), 0.0)
+                    + jnp.where(lane == COLS - 1, shift(first, COLS - 1 - t), 0.0)
+                )
+                if i == 0 and heat is not None:
+                    cols = jnp.where(near_edge, shift(heat_cols, -4 * r), 0.0)
+                    value = value + (heat_rows[r] + cols)
+                values[own].append(value)
+        for own in range(2):
+
+            @pl.when(at_rim[own] == 0)
+            def _(own=own):
+                for i in range(3):
+                    send_ns[k + 1, own, i] = values[own][i]
+                start(k + 1, par, False, own)
+
+        send_found_cols(k + 1, par, False, patch)
 
     def or_zero(r):
         return heat_row(r) if 0 <= r < ROWS else zero

time: 39.1 us -> 38.6 us (0.987)
  Pallas kernels: 38.3 us -> 37.8 us
    pallas_call x1, Pallas kernels: 37.5 us -> 37 us  [pinned(): step(*(pltpu.with_memory_space_constraint(a, pltpu.HBM) for a in args))]
where the time goes in v10:
time: 38.6 us; the launch traced here: 38.5 us
  Pallas kernels  37.8 us (98%)
  between operations  0.64 us (2%)
    pallas_call x1, Pallas kernels, pinned(): step(*(pltpu.with_memory_space_constraint(a, pltpu.HBM) for a in args))  37 us
    pallas_call x1, Pallas kernels, on_device(): place(*pinned(heat.reshape(heat_shape.shape), flow.reshape(flow_shape.sha...  0.82 us

profile of v10, /device:TPU:6, one launch (start us, length us, event | category | flops | bytes accessed | tf_op | source)
XLA Modules:
  0.0 38.5 jit_solution(796632439341394834)
XLA Ops:
  0.6 37.0 %mantle_step.1 = (f32[32,8,128]{2,1,0:T(8,128)S(1)}, f32[32,3,8,128]{3,2,1,0:T(8,128)S(1)}, f32[8,8,128]{2,1,0:T(8,128)S(1)}) custom-call(f32[8,32,128]{2,1,0:T(8,128)} %bitcast.5, f32[3,8,32,128]{3,2,1,0:T(8,128)} %bitcast.4, f32[8]{0:T(128)} %refs_2_.1, s32[1,1,640]{2,1,0:T(1,128)} %refs_3_.1, f32[1,1,320]{2,1,0:T(1,128)} %refs_4_.1), custom_call_target="tpu_custom_call" | custom-call | tf_op jit(solution)/shard_map/mantle_step/pallas_call | solution.py:520
  37.7 0.8 %deliver.1 = (f32[8,32,128]{2,1,0:T(8,128)}, f32[3,8,32,128]{3,2,1,0:T(8,128)}) custom-call(f32[32,8,128]{2,1,0:T(8,128)S(1)} %get-tuple-element.7.heat_in, f32[32,3,8,128]{3,2,1,0:T(8,128)S(1)} %get-tuple-element.8.flow_in, f32[8,8,128]{2,1,0:T(8,128)S(1)} %get-tuple-element.9.halo_in), custom_call_target="tpu_custom_call" | custom-call | tf_op jit(solution)/shard_map/deliver/pallas_call | solution.py:523

commit v11 on v10

--- a/solution.py
+++ b/solution.py
@@ -142,6 +142,20 @@
             device_id_type=MESH,
         )
 
+    def start_rim(k, par, first, ns):
+        side = south if ns else east
+        buf, halo = (send_ns, halo_ns) if ns else (send_we, halo_we)
+        n = (5 if first else 3) if ns else (2 if first else 1)
+        at = side if ns else side + 2
+        pltpu.make_async_remote_copy(
+            src_ref=buf.at[k, side, 0:n],
+            dst_ref=halo.at[k, side, 0:n],
+            send_sem=send_sem.at[par, at],
+            recv_sem=recv_sem.at[par, at],
+            device_id=(1 - p, c, l),
+            device_id_type=MESH,
+        ).start()
+
     def on_rim(flag_a, flag_b):
         return pl.when((flag_a == 1) | (flag_b == 1))
 
@@ -181,34 +195,17 @@
         return a, cos * b + sin * d, cos * d - sin * b
 
     def send_found_rows(k, par, first, patch):
-        @on_rim(north, south)
-        def _():
-            values = patch([found[i] for i in range(3)], ns_site)
-            for i, v in enumerate(rotated(values, 6)):
-                send_ns[k, south, i] = v
-
-            @pl.when(north == 1)
-            def _():
-                start(k, par, first, 0)
-
-            @pl.when(south == 1)
-            def _():
-                start(k, par, first, 1)
+        values = patch([found[i] for i in range(3)])
+        for i, v in enumerate(rotated(values, 6)):
+            send_ns[k, south, i] = v
+        start_rim(k, par, first, True)
 
     def send_found_cols(k, par, first, patch):
         @on_rim(west, east)
         def _():
-            values = patch([found[3 + i] for i in range(3)], we_site)
-            a, b, d = rotated(values, 8)
+            a, b, d = rotated(patch([found[3 + i] for i in range(3)]), 8)
             send_we[k, east, 0] = jnp.where(slot_part == 0, a, jnp.where(slot_part == 1, b, d))
-
-            @pl.when(west == 1)
-            def _():
-                start(k, par, first, 2)
-
-            @pl.when(east == 1)
-            def _():
-                start(k, par, first, 3)
+            start_rim(k, par, first, False)
 
     def send_inside(k, par, first, which=(2, 3, 0, 1)):
         for side in which:
@@ -257,8 +254,12 @@
     find(flow_row)
     pl.semaphore_wait(barrier, 4)
     send_inside(0, 0, True)
-    send_found_rows(0, 0, True, lambda values, index: values)
-    send_found_cols(0, 0, True, lambda values, index: values)
+
+    @on_rim(north, south)
+    def _():
+        send_found_rows(0, 0, True, lambda values: values)
+
+    send_found_cols(0, 0, True, lambda values: values)
 
     def relax(rows, source=None, result=flow):
         before = [zero] * 3
@@ -293,6 +294,19 @@
         return with_halo(lambda r, i: flow[r, i], halo_share(k), on_edge)
 
     def send_edges(k, par, even, odd, heat=None):
+        on_side = north + south
+
+        @pl.when(on_side == 1)
+        def _():
+            send_edges_as(True, k, par, even, odd, heat)
+
+        @pl.when(on_side == 0)
+        def _():
+            send_edges_as(False, k, par, even, odd, heat)
+
+    def send_edges_as(rim, k, par, even, odd, heat):
+        if heat is None:
+            wait_all(k, 1 - par, False, (0, 1))
         above = [coef * halo_ns[k, 0, i] for i in range(3)]
         below = [coef * halo_ns[k, 1, i] for i in range(3)]
         for i in range(3):
@@ -303,8 +317,35 @@
             for r, value in heat_rows.items():
                 part = shift(jnp.where(on_edge, value, 0.0), r)
                 even, odd = (even, odd + part) if r & 1 else (even + part, odd)
+        def patch_rows(index):
+            at_row, at_col = index >> 7, index & (COLS - 1)
+            adds = []
+            for i in range(3):
+                add = jnp.where(at_row == 0, lane_take(above[i], at_col), 0.0)
+                add = add + jnp.where(at_row == ROWS - 1, lane_take(below[i], at_col), 0.0)
+                if i == 0 and heat is not None:
+                    for r, value in heat_rows.items():
+                        add = add + jnp.where(at_row == r, lane_take(value, at_col), 0.0)
+                    near = (at_col < 2) | (at_col >= COLS - 2)
+                    cols = lane_take(heat_cols, (4 * at_row + at_col) & (COLS - 1))
+                    add = add + jnp.where(near, cols, 0.0)
+                adds.append(add)
+            return adds
+
+        def patch_cols(index, adds):
+            at_row, at_col = index >> 7, index & (COLS - 1)
+            adds = list(adds)
+            for i in range(3):
+                slot = i * ROWS + at_row
+                add = jnp.where(at_col == 0, lane_take(last, slot), 0.0)
+                add = add + jnp.where(at_col == COLS - 1, lane_take(first, slot), 0.0)
+                adds[i] = adds[i] + add
+            return adds
+
         west_edge, east_edge = jnp.where(is_even, even, odd), shift(jnp.where(is_even, odd, even), 1)
         outer = [[flow[0, i] + above[i] for i in range(3)], [flow[ROWS - 1, i] + below[i] for i in range(3)]]
+        if rim:
+            adds = patch_rows(ns_site)
         if heat is None:
             wait_all(k, 1 - par, False, (2, 3))
         last, first = coef * halo_we[k, 0, 0], coef * halo_we[k, 1, 0]
@@ -318,24 +359,9 @@
         send_we[k + 1, 1, 0] = east_edge + to_east
         send_inside(k + 1, par, False, (2, 3))
 
-        def patch(values, index):
-            at_row, at_col = index >> 7, index & (COLS - 1)
-            for i in range(3):
-                slot = i * ROWS + at_row
-                add = jnp.where(at_row == 0, lane_take(above[i], at_col), 0.0)
-                add = add + jnp.where(at_row == ROWS - 1, lane_take(below[i], at_col), 0.0)
-                add = add + jnp.where(at_col == 0, lane_take(last, slot), 0.0)
-                add = add + jnp.where(at_col == COLS - 1, lane_take(first, slot), 0.0)
-                if i == 0 and heat is not None:
-                    for r, value in heat_rows.items():
-                        add = add + jnp.where(at_row == r, lane_take(value, at_col), 0.0)
-                    near = (at_col < 2) | (at_col >= COLS - 2)
-                    cols = lane_take(heat_cols, (4 * at_row + at_col) & (COLS - 1))
-                    add = add + jnp.where(near, cols, 0.0)
-                values[i] = values[i] + add
-            return values
-
-        send_found_rows(k + 1, par, False, patch)
+        if rim:
+            adds = patch_cols(ns_site, adds)
+            send_found_rows(k + 1, par, False, lambda found: [f + add for f, add in zip(found, adds)])
         values = ([], [])
         for own, r in ((0, 0), (1, ROWS - 1)):
             for i in range(3):
@@ -356,6 +382,11 @@
                 for i in range(3):
                     send_ns[k + 1, own, i] = values[own][i]
                 start(k + 1, par, False, own)
+
+
+        def patch(found):
+            adds = patch_cols(we_site, patch_rows(we_site))
+            return [f + add for f, add in zip(found, adds)]
 
         send_found_cols(k + 1, par, False, patch)
 
@@ -432,7 +463,6 @@
         def _():
             wait_sent(k - 1, 1 - par, False)
 
-        wait_all(k, par, False, (0, 1))
         send_edges(k, 1 - par, even, odd)
         return carry
 

time: 38.6 us -> 38.6 us (level)
  no operation moved by 1% of the time
where the time goes in v11:
time: 38.6 us; the launch traced here: 38.5 us
  Pallas kernels  37.8 us (98%)
  between operations  0.64 us (2%)
    pallas_call x1, Pallas kernels, pinned(): step(*(pltpu.with_memory_space_constraint(a, pltpu.HBM) for a in args))  37 us
    pallas_call x1, Pallas kernels, on_device(): place(*pinned(heat.reshape(heat_shape.shape), flow.reshape(flow_shape.sha...  0.82 us

profile of v11, /device:TPU:6, one launch (start us, length us, event | category | flops | bytes accessed | tf_op | source)
XLA Modules:
  0.0 38.5 jit_solution(7958417222632465520)
XLA Ops:
  0.6 37.0 %mantle_step.1 = (f32[32,8,128]{2,1,0:T(8,128)S(1)}, f32[32,3,8,128]{3,2,1,0:T(8,128)S(1)}, f32[8,8,128]{2,1,0:T(8,128)S(1)}) custom-call(f32[8,32,128]{2,1,0:T(8,128)} %bitcast.5, f32[3,8,32,128]{3,2,1,0:T(8,128)} %bitcast.4, f32[8]{0:T(128)} %refs_2_.1, s32[1,1,640]{2,1,0:T(1,128)} %refs_3_.1, f32[1,1,320]{2,1,0:T(1,128)} %refs_4_.1), custom_call_target="tpu_custom_call" | custom-call | tf_op jit(solution)/shard_map/mantle_step/pallas_call | solution.py:550
  37.7 0.8 %deliver.1 = (f32[8,32,128]{2,1,0:T(8,128)}, f32[3,8,32,128]{3,2,1,0:T(8,128)}) custom-call(f32[32,8,128]{2,1,0:T(8,128)S(1)} %get-tuple-element.7.heat_in, f32[32,3,8,128]{3,2,1,0:T(8,128)S(1)} %get-tuple-element.8.flow_in, f32[8,8,128]{2,1,0:T(8,128)S(1)} %get-tuple-element.9.halo_in), custom_call_target="tpu_custom_call" | custom-call | tf_op jit(solution)/shard_map/deliver/pallas_call | solution.py:553

commit v12 on v11

--- a/solution.py
+++ b/solution.py
@@ -142,6 +142,22 @@
             device_id_type=MESH,
         )
 
+    def start_columns(k, par, first):
+        n = 2 if first else 1
+        far = (lax.rem(l, 8) == 7).astype(jnp.int32)
+        for own in (far, 1 - far):
+
+            @pl.when(west + own * (east - west) == 0)
+            def _(own=own):
+                pltpu.make_async_remote_copy(
+                    src_ref=send_we.at[k, own, 0:n],
+                    dst_ref=halo_we.at[k, 1 - own, 0:n],
+                    send_sem=send_sem.at[par, 2 + own],
+                    recv_sem=recv_sem.at[par, 3 - own],
+                    device_id=(p, c, l - 1 + 2 * own),
+                    device_id_type=MESH,
+                ).start()
+
     def start_rim(k, par, first, ns):
         side = south if ns else east
         buf, halo = (send_ns, halo_ns) if ns else (send_we, halo_we)
@@ -252,12 +268,20 @@
         send_we[0, east, 1] = collect(we_heat, lambda r, _: heat_row(r), 1)[0]
 
     find(flow_row)
-    pl.semaphore_wait(barrier, 4)
-    send_inside(0, 0, True)
 
     @on_rim(north, south)
     def _():
-        send_found_rows(0, 0, True, lambda values: values)
+        for i, v in enumerate(rotated([found[i] for i in range(3)], 6)):
+            send_ns[0, south, i] = v
+
+    pl.semaphore_wait(barrier, 4)
+
+    @on_rim(north, south)
+    def _():
+        start_rim(0, 0, True, True)
+
+    start_columns(0, 0, True)
+    send_inside(0, 0, True, (0, 1))
 
     send_found_cols(0, 0, True, lambda values: values)
 
@@ -357,7 +381,7 @@
             to_east = to_east + jnp.where(lane < ROWS, at_last, 0.0)
         send_we[k + 1, 0, 0] = west_edge + to_west
         send_we[k + 1, 1, 0] = east_edge + to_east
-        send_inside(k + 1, par, False, (2, 3))
+        start_columns(k + 1, par, False)
 
         if rim:
             adds = patch_cols(ns_site, adds)

time: 38.6 us -> 38.6 us (level)
  no operation moved by 1% of the time
where the time goes in v12:
time: 38.6 us; the launch traced here: 38.5 us
  Pallas kernels  37.8 us (98%)
  between operations  0.64 us (2%)
    pallas_call x1, Pallas kernels, pinned(): step(*(pltpu.with_memory_space_constraint(a, pltpu.HBM) for a in args))  37 us
    pallas_call x1, Pallas kernels, on_device(): place(*pinned(heat.reshape(heat_shape.shape), flow.reshape(flow_shape.sha...  0.82 us

profile of v12, /device:TPU:6, one launch (start us, length us, event | category | flops | bytes accessed | tf_op | source)
XLA Modules:
  0.0 38.5 jit_solution(15701259992123439263)
XLA Ops:
  0.6 37.0 %mantle_step.1 = (f32[32,8,128]{2,1,0:T(8,128)S(1)}, f32[32,3,8,128]{3,2,1,0:T(8,128)S(1)}, f32[8,8,128]{2,1,0:T(8,128)S(1)}) custom-call(f32[8,32,128]{2,1,0:T(8,128)} %bitcast.5, f32[3,8,32,128]{3,2,1,0:T(8,128)} %bitcast.4, f32[8]{0:T(128)} %refs_2_.1, s32[1,1,640]{2,1,0:T(1,128)} %refs_3_.1, f32[1,1,320]{2,1,0:T(1,128)} %refs_4_.1), custom_call_target="tpu_custom_call" | custom-call | tf_op jit(solution)/shard_map/mantle_step/pallas_call | solution.py:574
  37.7 0.8 %deliver.1 = (f32[8,32,128]{2,1,0:T(8,128)}, f32[3,8,32,128]{3,2,1,0:T(8,128)}) custom-call(f32[32,8,128]{2,1,0:T(8,128)S(1)} %get-tuple-element.7.heat_in, f32[32,3,8,128]{3,2,1,0:T(8,128)S(1)} %get-tuple-element.8.flow_in, f32[8,8,128]{2,1,0:T(8,128)S(1)} %get-tuple-element.9.halo_in), custom_call_target="tpu_custom_call" | custom-call | tf_op jit(solution)/shard_map/deliver/pallas_call | solution.py:577

commit v13 on v11

--- a/solution.py
+++ b/solution.py
@@ -252,12 +252,19 @@
         send_we[0, east, 1] = collect(we_heat, lambda r, _: heat_row(r), 1)[0]
 
     find(flow_row)
-    pl.semaphore_wait(barrier, 4)
-    send_inside(0, 0, True)
 
     @on_rim(north, south)
     def _():
-        send_found_rows(0, 0, True, lambda values: values)
+        for i, v in enumerate(rotated([found[i] for i in range(3)], 6)):
+            send_ns[0, south, i] = v
+
+    pl.semaphore_wait(barrier, 4)
+
+    @on_rim(north, south)
+    def _():
+        start_rim(0, 0, True, True)
+
+    send_inside(0, 0, True)
 
     send_found_cols(0, 0, True, lambda values: values)
 

time: 38.6 us -> 38.6 us (level)
  no operation moved by 1% of the time
where the time goes in v13:
time: 38.6 us; the launch traced here: 38.5 us
  Pallas kernels  37.9 us (98%)
  between operations  0.64 us (2%)
    pallas_call x1, Pallas kernels, pinned(): step(*(pltpu.with_memory_space_constraint(a, pltpu.HBM) for a in args))  37 us
    pallas_call x1, Pallas kernels, on_device(): place(*pinned(heat.reshape(heat_shape.shape), flow.reshape(flow_shape.sha...  0.82 us

profile of v13, /device:TPU:6, one launch (start us, length us, event | category | flops | bytes accessed | tf_op | source)
XLA Modules:
  0.0 38.5 jit_solution(845334711103173289)
XLA Ops:
  0.6 37.0 %mantle_step.1 = (f32[32,8,128]{2,1,0:T(8,128)S(1)}, f32[32,3,8,128]{3,2,1,0:T(8,128)S(1)}, f32[8,8,128]{2,1,0:T(8,128)S(1)}) custom-call(f32[8,32,128]{2,1,0:T(8,128)} %bitcast.5, f32[3,8,32,128]{3,2,1,0:T(8,128)} %bitcast.4, f32[8]{0:T(128)} %refs_2_.1, s32[1,1,640]{2,1,0:T(1,128)} %refs_3_.1, f32[1,1,320]{2,1,0:T(1,128)} %refs_4_.1), custom_call_target="tpu_custom_call" | custom-call | tf_op jit(solution)/shard_map/mantle_step/pallas_call | solution.py:557
  37.7 0.8 %deliver.1 = (f32[8,32,128]{2,1,0:T(8,128)}, f32[3,8,32,128]{3,2,1,0:T(8,128)}) custom-call(f32[32,8,128]{2,1,0:T(8,128)S(1)} %get-tuple-element.7.heat_in, f32[32,3,8,128]{3,2,1,0:T(8,128)S(1)} %get-tuple-element.8.flow_in, f32[8,8,128]{2,1,0:T(8,128)S(1)} %get-tuple-element.9.halo_in), custom_call_target="tpu_custom_call" | custom-call | tf_op jit(solution)/shard_map/deliver/pallas_call | solution.py:560

commit v14 on v11

--- a/solution.py
+++ b/solution.py
@@ -487,7 +487,7 @@
     def send(r):
         pltpu.make_async_copy(done.at[r], flow_out.at[:, :, r, :], sem.at[1]).start()
 
-    lag = 4
+    lag = 2
     for r in range(ROWS):
         for i in range(3):
             done[r, i] = rows(r, i)

time: 38.6 us -> 38.6 us (level)
  no operation moved by 1% of the time
where the time goes in v14:
time: 38.6 us; the launch traced here: 38.5 us
  Pallas kernels  37.8 us (98%)
  between operations  0.64 us (2%)
    pallas_call x1, Pallas kernels, pinned(): step(*(pltpu.with_memory_space_constraint(a, pltpu.HBM) for a in args))  37 us
    pallas_call x1, Pallas kernels, on_device(): place(*pinned(heat.reshape(heat_shape.shape), flow.reshape(flow_shape.sha...  0.81 us

profile of v14, /device:TPU:6, one launch (start us, length us, event | category | flops | bytes accessed | tf_op | source)
XLA Modules:
  0.0 38.5 jit_solution(5522783558629911741)
XLA Ops:
  0.6 37.0 %mantle_step.1 = (f32[32,8,128]{2,1,0:T(8,128)S(1)}, f32[32,3,8,128]{3,2,1,0:T(8,128)S(1)}, f32[8,8,128]{2,1,0:T(8,128)S(1)}) custom-call(f32[8,32,128]{2,1,0:T(8,128)} %bitcast.5, f32[3,8,32,128]{3,2,1,0:T(8,128)} %bitcast.4, f32[8]{0:T(128)} %refs_2_.1, s32[1,1,640]{2,1,0:T(1,128)} %refs_3_.1, f32[1,1,320]{2,1,0:T(1,128)} %refs_4_.1), custom_call_target="tpu_custom_call" | custom-call | tf_op jit(solution)/shard_map/mantle_step/pallas_call | solution.py:550
  37.7 0.8 %deliver.1 = (f32[8,32,128]{2,1,0:T(8,128)}, f32[3,8,32,128]{3,2,1,0:T(8,128)}) custom-call(f32[32,8,128]{2,1,0:T(8,128)S(1)} %get-tuple-element.7.heat_in, f32[32,3,8,128]{3,2,1,0:T(8,128)S(1)} %get-tuple-element.8.flow_in, f32[8,8,128]{2,1,0:T(8,128)S(1)} %get-tuple-element.9.halo_in), custom_call_target="tpu_custom_call" | custom-call | tf_op jit(solution)/shard_map/deliver/pallas_call | solution.py:553
